TPU v7x, 32 devices: a whole 2x2x4 slice. The times are simulated.
32 devices in a mesh: group: 2 (over y), shard: 16 (over z, x, core).
Axes of the slice: x: 2, y: 2, z: 4, core: 2. Of those that a mesh axis runs over, the one named last changes fastest.
Arguments:
- samples: bfloat16 [32, 8192], P('shard'), may hold values from -6 to 6
- factor_old: float32 [8192, 8192], P('shard', 'group'), as said below
- damping: float32 [1], replicated, may hold values from 0.1 to 1
- gradients: bfloat16 [2048, 8192], P('shard', 'group'), may hold values from -6 to 6
Outputs:
- swept_factor: float32 [8192, 8192], P('shard', 'group')
- update: bfloat16 [8192, 2048], P('shard', 'group')
Inputs may be any that keep to these rules, and one draw needn't show every extreme that they name: factor_old is symmetric and positive definite.
All inputs are finite; a program needn't handle non-finite values.
Results may differ from a plain program's by a relative error of at most 0.0049.
Values may be sent and summed in bfloat16 or wider, within the bound.
A program may use at most 128 MiB of HBM per device.

v0:
```python
import jax
import jax.numpy as jnp
from jax import lax
from jax.sharding import PartitionSpec as P

D = 8192
BLOCK = 128
PIVOTS = 2


ema_keep = 0.5


def spread(block, axis, holder):
    block = jnp.where(lax.axis_index(axis) == holder, block, jnp.zeros_like(block))
    return lax.psum(block, axis)


def solve_spd(pivot_block, right_side):
    lower_factor = jnp.linalg.cholesky(pivot_block)
    half_solved = lax.linalg.triangular_solve(lower_factor, right_side, left_side=True, lower=True)
    return lax.linalg.triangular_solve(
        lower_factor, half_solved, left_side=True, lower=True, transpose_a=True
    )


def on_device(samples, factor_old, damping, gradients):
    row_count, col_count = factor_old.shape
    shard_index = lax.axis_index("shard")
    group_index = lax.axis_index("group")
    row_first = shard_index * row_count
    col_first = group_index * col_count
    total_tokens = samples.shape[0] * lax.axis_size("shard")
    contract = (((0,), (0,)), ((), ()))
    token_piece = lax.all_gather(samples, "shard", axis=0, tiled=True)
    left_part = lax.dynamic_slice_in_dim(token_piece, row_first, row_count, 1)
    right_part = lax.dynamic_slice_in_dim(token_piece, col_first, col_count, 1)
    covariance = lax.dot_general(
        left_part, right_part, contract, preferred_element_type=jnp.float32
    )
    row_ids = lax.broadcasted_iota(jnp.int32, (row_count, col_count), 0) + row_first
    col_ids = lax.broadcasted_iota(jnp.int32, (row_count, col_count), 1) + col_first
    diagonal = jnp.where(row_ids == col_ids, damping[0], 0.0)
    factor = ema_keep * factor_old + (1.0 - ema_keep) * (covariance / total_tokens) + diagonal
    spacing = D // PIVOTS
    sel_rows = lax.broadcasted_iota(jnp.int32, (BLOCK, col_count), 0)
    sel_cols = lax.broadcasted_iota(jnp.int32, (BLOCK, col_count), 1) + col_first

    def sweep_once(sweep_step, matrix):
        first_index = (sweep_step * spacing).astype(jnp.int32)
        col_owner = first_index // col_count
        row_owner = first_index // row_count
        col_offset = first_index - col_owner * col_count
        row_offset = first_index - row_owner * row_count
        own_columns = lax.dynamic_slice_in_dim(matrix, col_offset, BLOCK, 1)
        column = spread(own_columns, "group", col_owner)
        own_rows = lax.dynamic_slice_in_dim(matrix, row_offset, BLOCK, 0)
        own_pivot = lax.dynamic_slice_in_dim(column, row_offset, BLOCK, 0)
        pivot_strip, pivot_block = (
            spread(own_rows, "shard", row_owner),
            spread(own_pivot, "shard", row_owner),
        )
        selector = jnp.where(sel_cols == sel_rows + first_index, 1.0, 0.0).astype(jnp.float32)
        factor_q = solve_spd(pivot_block, pivot_strip + selector)
        matrix = matrix - jnp.dot(
            column, factor_q, precision=lax.Precision.HIGHEST, preferred_element_type=jnp.float32
        )
        addition = jnp.where(shard_index == row_owner, factor_q, 0.0)
        block_rows = lax.dynamic_slice_in_dim(matrix, row_offset, BLOCK, 0) + addition
        return lax.dynamic_update_slice_in_dim(matrix, block_rows, row_offset, 0)

    swept_factor = lax.fori_loop(0, PIVOTS, sweep_once, factor)
    swept_half = swept_factor.astype(jnp.bfloat16)
    partial_terms = lax.dot_general(
        swept_half,
        lax.all_gather(gradients, "shard", axis=0, tiled=True),
        (((1,), (1,)), ((), ())),
        preferred_element_type=jnp.float32,
    )
    update = lax.psum_scatter(partial_terms, "group", scatter_dimension=1, tiled=True).astype(
        jnp.bfloat16
    )
    return (swept_factor, update)


def damped(old, left, right, total, hit, damping):
    cov = lax.dot_general(left, right, (((0,), (0,)), ((), ())), preferred_element_type=jnp.float32)
    return ema_keep * old + (1.0 - ema_keep) * (cov / total) + jnp.where(hit, damping, 0.0)


def exact(a, b):
    return jnp.dot(a, b, precision=lax.Precision.HIGHEST, preferred_element_type=jnp.float32)


def on_device_pairs(samples, factor_old, damping, gradients):
    rows, cols = factor_old.shape
    shards = lax.axis_size("shard")
    shard = lax.axis_index("shard")
    group = lax.axis_index("group")
    row_first, col_first = shard * rows, group * cols
    total = samples.shape[0] * shards
    wide = PIVOTS * BLOCK
    bf16, f32 = jnp.bfloat16, jnp.float32
    half_count = shards // PIVOTS
    shard_half = shard // half_count
    own = factor_old[:, :BLOCK]
    high = own.astype(bf16)
    low = (own[:BLOCK] - high[:BLOCK].astype(f32)).astype(bf16)
    swap = [(0, 1), (1, 0)]

    def ordered(first, mine, other, axis):
        return jnp.concatenate([jnp.where(first, mine, other), jnp.where(first, other, mine)], axis=axis)

    mine = jnp.concatenate([high, low], axis=0)
    pair = ordered(group == 0, mine, lax.ppermute(mine, "group", swap), 1)
    across = [(i, i ^ half_count) for i in range(shards)]
    tokens = jnp.concatenate([samples, lax.ppermute(samples, "shard", across)], axis=0).reshape(-1, wide)
    one_way = [(g * shards + i, g * shards + (i ^ half_count))
               for g in range(PIVOTS) for i in range(shards) if i // half_count == g]
    moved = lax.ppermute(pair, ("group", "shard"), one_way)
    held = jnp.concatenate([jnp.where(shard_half == group, pair, moved), tokens], axis=0)[None]
    bits = [1 << k for k in range(half_count.bit_length() - 1)]
    bits = bits[1:] + bits[:1]
    for bit in bits:
        other = lax.ppermute(held, "shard", [(i, i ^ bit) for i in range(shards)])
        held = ordered((shard & bit) == 0, held, other, 0)
    depth = held.shape[1]
    held = jnp.swapaxes(held.reshape(2, half_count // 2, depth, wide), 0, 1)
    held = held.reshape(half_count, depth, wide)
    units = gradients.shape[0] // 2
    gathered = []
    for half in range(2):
        piece = gradients[half * units:(half + 1) * units]
        gathered.append(lax.all_gather(piece, "shard", axis=0, tiled=False))
    tokens = held[:, rows + BLOCK:].reshape(total, D)
    columns = held[:, :rows].reshape(cols, wide)
    spacing = D // PIVOTS
    ptok = jnp.concatenate([tokens[:, p * spacing:p * spacing + BLOCK] for p in range(PIVOTS)], axis=1)
    pidx = jnp.concatenate([jnp.arange(BLOCK) + p * spacing for p in range(PIVOTS)])
    left = lax.dynamic_slice_in_dim(tokens, row_first, rows, 1)
    right = lax.dynamic_slice_in_dim(tokens, col_first, cols, 1)
    rid = jnp.arange(rows) + row_first
    cid = jnp.arange(cols) + col_first
    d0 = damping[0]
    col_own = pair[:rows].astype(f32)
    C = damped(col_own, left, ptok, total, rid[:, None] == pidx[None, :], d0)
    strip = columns.T.astype(f32)
    R = damped(strip, ptok, right, total, pidx[:, None] == cid[None, :], d0)
    tops = jnp.stack([held[0, :BLOCK], held[0, rows:rows + BLOCK]])
    tops = ordered(group == 0, tops, lax.ppermute(tops, "group", swap), 1).astype(f32)
    A = damped(tops[0] + tops[1], ptok, ptok, total, pidx[:, None] == pidx[None, :], d0)
    E = jnp.where(pidx[:, None] == cid[None, :], 1.0, 0.0).astype(f32)
    ones = jnp.eye(BLOCK, dtype=f32)
    a, b = slice(0, BLOCK), slice(BLOCK, wide)
    inv1 = solve_spd(A[a, a], ones)
    q1 = exact(inv1, R[a] + E[a])
    cross = exact(inv1, A[a, b])
    A22 = A[b, b] - exact(A[b, a], cross)
    inv2 = solve_spd(A22, ones)
    q2 = exact(inv2, R[b] - exact(A[b, a], q1) + E[b])
    rows1 = shard == 0
    C2 = C[:, b] - exact(C[:, a], cross)
    add = jnp.where(rows1, cross, 0.0)
    C2 = C2.at[:BLOCK].add(add)
    Q = jnp.concatenate([q1, q2], axis=0)
    both = jnp.concatenate([C[:, a], C2], axis=1)
    factor = damped(factor_old, left, right, total, rid[:, None] == cid[None, :], d0)
    swept = factor - jnp.dot(both, Q, precision=lax.Precision.HIGH, preferred_element_type=f32)
    owner2 = spacing // rows
    extra = jnp.where(rows1, q1, jnp.where(shard == owner2, q2, 0.0))
    swept = swept.at[:BLOCK].add(extra)
    half_swept = swept.astype(bf16)
    out = []
    for g in gathered:
        piece = g.reshape(-1, cols)
        width = piece.shape[0] // PIVOTS
        part = lax.dot_general(half_swept, piece, (((1,), (1,)), ((), ())), preferred_element_type=f32)
        theirs = lax.dynamic_slice_in_dim(part, (1 - group) * width, width, 1).astype(bf16)
        sent = lax.ppermute(theirs, "group", swap)
        ours = lax.dynamic_slice_in_dim(part, group * width, width, 1)
        out.append((ours + sent.astype(f32)).astype(bf16).reshape(rows, half_count, 1, units))
    update = jnp.concatenate(out, axis=2).reshape(rows, -1)
    return (swept, update)


def solution(mesh):
    sizes = dict(mesh.shape)
    paired = sizes["group"] == PIVOTS == 2 and D // sizes["shard"] >= BLOCK
    paired = paired and sizes["shard"] >= 4 and sizes["shard"] & (sizes["shard"] - 1) == 0
    return jax.shard_map(
        on_device_pairs if paired else on_device,
        mesh=mesh,
        in_specs=(P("shard", None), P("shard", "group"), P(), P("shard", "group")),
        out_specs=(P("shard", "group"), P("shard", "group")),
        check_vma=False,
    )
```

profile of v0, /device:TPU:0, one launch (start us, length us, event | category | flops | bytes accessed | tf_op | source)
XLA Modules:
  0.0 268.7 jit_solution(15548467931142751032)
XLA Ops:
  7.2 2.3 fusion.57
  9.6 9.0 %copy.14 = f32[512,4096]{0,1:T(8,128)} copy(f32[512,4096]{1,0:T(8,128)} %param.14) | data formatting | bytes 16777216 | tf_op args[1]
  18.5 4.3 %convert.3 = bf16[512,4096]{0,1:T(8,128)(2,1)S(1)} convert(f32[512,4096]{0,1:T(8,128)} %copy.14) | non-fusion elementwise | flops 2097152 | bytes 12582912 | tf_op jit(solution)/shard_map/convert
  23.8 3.0 %collective-permute-start = (bf16[640,128]{0,1:T(8,128)(2,1)S(1)}, bf16[640,128]{0,1:T(8,128)(2,1)S(1)}, u32[]{:S(2)}, u32[]{:S(2)}) collective-permute-start(bf16[640,128]{0,1:T(8,128)(2,1)S(1)} %pad_maximum_fusion.5), channel_id=1, source_target_pairs={{0,16},{16,0},{1,17},{17,1},{2,18},{18,2},{3,19},{19,3},{4,20},{20... | collective-permute-start | bytes 491528 | tf_op jit(solution)/shard_map/ppermute | solution.py:115
  26.8 2.6 collective-permute-start.2
  31.2 4.7 %collective-permute-start.1 = (bf16[640,256]{0,1:T(8,128)(2,1)S(1)}, bf16[640,256]{0,1:T(8,128)(2,1)S(1)}, u32[]{:S(2)}, u32[]{:S(2)}) collective-permute-start(bf16[640,256]{0,1:T(8,128)(2,1)S(1)} %pad_maximum_fusion.4), channel_id=1, source_target_pairs={{0,8},{1,9},{2,10},{3,11},{4,12},{5,13},{6,14},{7,15},{24,16},{25,... | collective-permute-start | bytes 983048 | tf_op jit(solution)/shard_map/ppermute | solution.py:120
  36.2 10.2 %collective-permute-done.1 = bf16[640,256]{0,1:T(8,128)(2,1)S(1)} collective-permute-done((bf16[640,256]{0,1:T(8,128)(2,1)S(1)}, bf16[640,256]{0,1:T(8,128)(2,1)S(1)}, u32[]{:S(2)}, u32[]{:S(2)}) %collective-permute-start.1) | collective-permute-done | bytes 327712 | tf_op jit(solution)/shard_map/ppermute | solution.py:120
  48.2 8.7 %collective-permute-done.3 = bf16[1,768,256]{1,2,0:T(8,128)(2,1)S(1)} collective-permute-done((bf16[1,768,256]{1,2,0:T(8,128)(2,1)S(1)}, bf16[1,768,256]{1,2,0:T(8,128)(2,1)S(1)}, u32[]{:S(2)}, u32[]{:S(2)}) %collective-permute-start.3) | collective-permute-done | bytes 393248 | tf_op jit(solution)/shard_map/ppermute | solution.py:125
  57.2 16.4 %collective-permute-start.4 = (bf16[2,768,256]{1,2,0:T(8,128)(2,1)S(1)}, bf16[2,768,256]{1,2,0:T(8,128)(2,1)}, u32[]{:S(2)}, u32[]{:S(2)}) collective-permute-start(bf16[2,768,256]{1,2,0:T(8,128)(2,1)S(1)} %pad_maximum_fusion.3), channel_id=1, source_target_pairs={{0,4},{1,5},{2,6},{3,7},{4,0},{5,1},{6,2},{7,3},{8,12},{9,13},{10,... | collective-permute-start | bytes 2359304 | tf_op jit(solution)/shard_map/ppermute | solution.py:125
  73.6 37.0 %collective-permute-done.4 = bf16[2,768,256]{1,2,0:T(8,128)(2,1)} collective-permute-done((bf16[2,768,256]{1,2,0:T(8,128)(2,1)S(1)}, bf16[2,768,256]{1,2,0:T(8,128)(2,1)}, u32[]{:S(2)}, u32[]{:S(2)}) %collective-permute-start.4) | collective-permute-done | bytes 786464 | tf_op jit(solution)/shard_map/ppermute | solution.py:125
  113.3 2.5 compare_select_fusion
  118.8 2.0 copy.18
  120.9 2.1 reshape.117
  124.2 2.7 %collective-permute-start.6 = (bf16[2,128,256]{1,2,0:T(8,128)(2,1)}, bf16[2,128,256]{1,2,0:T(8,128)(2,1)}, u32[]{:S(2)}, u32[]{:S(2)}) collective-permute-start(bf16[2,128,256]{1,2,0:T(8,128)(2,1)} %pad_maximum_fusion.6), channel_id=1, source_target_pairs={{0,16},{16,0},{1,17},{17,1},{2,18},{18,2},{3,19},{19,3},{4,20},{20... | collective-permute-start | bytes 393224 | tf_op jit(solution)/shard_map/ppermute | solution.py:150
  127.0 2.6 convert_multiply_fusion
  129.6 5.5 %copy.21 = f32[8,512,256]{2,1,0:T(8,128)} copy(f32[8,512,256]{1,2,0:T(8,128)} %convert_multiply_fusion) | data formatting | bytes 8388608 | tf_op jit(solution)/shard_map/mul | solution.py:88
  135.0 6.2 %copy.22 = f32[4096,256]{0,1:T(8,128)} copy(f32[4096,256]{1,0:T(8,128)} %bitcast.64) | data formatting | bytes 8388608 | tf_op jit(solution)/shard_map/mul | solution.py:88
  141.3 4.7 %fusion.24 = f32[512,4096]{1,0:T(8,128)} fusion(bf16[32,8192]{1,0:T(8,128)(2,1)S(1)} %copy-done.2, s32[]{:T(128)S(6)} %select_n.150, s32[]{:T(128)S(6)} %select_n.149), kind=kOutput, calls=%fused_computation.57 | convolution fusion | flops 134217728 | bytes 8683528 | tf_op jit(solution)/shard_map/dot_general | solution.py:87
  146.0 3.0 %fusion.1 = f32[256,4096]{1,0:T(8,128)} fusion(f32[4096,256]{0,1:T(8,128)S(1)} %copy-done.1, f32[]{:T(128)} %bitcast.61, s32[4096]{0:T(1024)S(1)} %iota_add_fusion, s32[256]{0:T(256)S(1)} %copy-done.9, bf16[32,8192]{1,0:T(8,128)(2,1)S(1)} %copy-done.2, s32[]{:T(128)S(6)} %select_n.150, bf16[32,128]{1,0:T(8,128)(2,1)S(1)} %get-tuple-element.42, ...), kind=kOutput, calls=%fused_computation.3 | convolution fusion | flops 72384512 | bytes 8684552 | tf_op jit(solution)/shard_map/dot_general | solution.py:87
  150.8 11.7 %cholesky.44 = f32[128,128]{1,0:T(8,128)S(1)} custom-call(f32[128,128]{1,0:T(8,128)S(1)} %fusion.43), custom_call_target="Cholesky" | custom-call | tf_op jit(solution)/shard_map/jit(cholesky)/cholesky | solution.py:20
  164.0 9.8 %custom-call.11 = f32[1,128,128]{1,2,0:T(8,128)S(1)} custom-call(f32[1,128,128]{2,1,0:T(8,128)S(1)} %fusion.30), custom_call_target="InvertDiagBlocksLowerTriangular" | custom-call | tf_op jit(solution)/shard_map/triangular_solve/custom-call.2 | solution.py:22
  174.9 11.9 %cholesky.55 = f32[128,128]{1,0:T(8,128)S(1)} custom-call(f32[128,128]{1,0:T(8,128)S(1)} %fusion.39), custom_call_target="Cholesky" | custom-call | tf_op jit(solution)/shard_map/jit(cholesky)/cholesky | solution.py:20
  188.2 9.8 %custom-call.13 = f32[1,128,128]{1,2,0:T(8,128)S(1)} custom-call(f32[1,128,128]{2,1,0:T(8,128)S(1)} %fusion.31), custom_call_target="InvertDiagBlocksLowerTriangular" | custom-call | tf_op jit(solution)/shard_map/triangular_solve/custom-call.2 | solution.py:22
  198.9 4.4 %fusion.7 = f32[128,4096]{1,0:T(8,128)S(1)} fusion(f32[128,128]{1,0:T(8,128)S(1)} %fusion.41, f32[256,4096]{1,0:T(8,128)} %compare_select_fusion, f32[256,4096]{1,0:T(8,128)} %fusion.1), kind=kOutput, calls=%fused_computation.16 | convolution fusion | flops 805830656 | bytes 6356992 | tf_op jit(solution)/shard_map/dot_general | solution.py:92
  203.3 3.9 %fusion.2 = f32[128,4096]{1,0:T(8,128)S(1)} fusion(f32[128,4096]{1,0:T(8,128)S(1)} %fusion.7, f32[256,4096]{1,0:T(8,128)} %compare_select_fusion, f32[256,4096]{1,0:T(8,128)S(1)} %copy-done, f32[256,256]{0,1:T(8,128)S(1)} %fusion.16), kind=kOutput, calls=%fused_computation.7 | convolution fusion | flops 806354944 | bytes 8454144 | tf_op jit(solution)/shard_map/dot_general | solution.py:92
  207.3 1.9 fusion.59
  209.3 10.1 %add_subtract_fusion = f32[512,4096]{1,0:T(8,128)} fusion(f32[512,4096]{1,0:T(8,128)S(1)} %bitcast.63, f32[512,4096]{1,0:T(8,128)} %param.14, f32[128,4096]{1,0:T(8,128)S(1)} %fusion.59, f32[128,4096]{1,0:T(8,128)S(1)} %fusion.7, f32[]{:T(128)} %bitcast.58, s32[4096]{0:T(1024)S(1)} %iota_add_fusion, s32[512]{0:T(512)S(1)} %copy-done.10, ...), kind=kOutput, calls=%fused_computation | convolution fusion | flops 3237085184 | bytes 29902852 | tf_op jit(solution)/shard_map/dot_general | solution.py:168
  219.4 3.3 %fusion.6 = f32[512,4096]{1,0:T(8,128)} fusion(f32[512,4096]{1,0:T(8,128)} %add_subtract_fusion, f32[128,4096]{1,0:T(8,128)S(1)} %fusion.7, f32[128,4096]{1,0:T(8,128)S(1)} %fusion.59, pred[]{:T(512)S(6)} %eq.105, pred[]{:T(512)S(6)} %eq.101), kind=kLoop, calls=%fused_computation.14 | loop fusion | flops 1572864 | bytes 8388610 | tf_op jit(solution)/shard_map/scatter-add | solution.py:171
  222.7 9.4 %fusion.11 = f32[512,1024]{1,0:T(8,128)S(1)} fusion(bf16[1024,4096]{1,0:T(8,128)(2,1)} %all-gather.5.cloned.1.call-done, f32[512,4096]{1,0:T(8,128)} %fusion.6), kind=kOutput, calls=%fused_computation.20 | convolution fusion | flops 4297064448 | bytes 18874368 | tf_op jit(solution)/shard_map/dot_general | solution.py:177
  232.4 9.5 %fusion.9 = f32[512,1024]{1,0:T(8,128)S(1)} fusion(bf16[1024,4096]{1,0:T(8,128)(2,1)} %all-gather.7.cloned.1.call-done, f32[512,4096]{1,0:T(8,128)} %fusion.6), kind=kOutput, calls=%fused_computation.18 | convolution fusion | flops 4297064448 | bytes 18874368 | tf_op jit(solution)/shard_map/dot_general | solution.py:177
  244.0 2.0 collective-permute-start.8
  246.7 11.6 %collective-permute-done.8 = bf16[512,512]{1,0:T(8,128)(2,1)} collective-permute-done((bf16[512,512]{1,0:T(8,128)(2,1)}, bf16[512,512]{1,0:T(8,128)(2,1)}, u32[]{:S(2)}, u32[]{:S(2)}) %collective-permute-start.8) | collective-permute-done | bytes 524320 | tf_op jit(solution)/shard_map/ppermute | solution.py:179
  (101 shorter events, 24.4 us)
Async XLA Ops:
  7.2 215.6 %all-gather.5.cloned.1.call-start = ((), (), s32[]{:S(2)}) async-start(), calls=%async_computation | async-start | bytes 8912896 | tf_op jit(solution)/shard_map/all_gather | solution.py:134
  9.5 222.8 %all-gather.7.cloned.1.call-start = ((), (), s32[]{:S(2)}) async-start(), calls=%async_computation.1 | async-start | bytes 8912896 | tf_op jit(solution)/shard_map/all_gather | solution.py:134
  18.5 8.3 %copy-start.7 = (bf16[2,8192]{1,0:T(2,128)(2,1)S(1)}, bf16[2,8192]{1,0:T(2,128)(2,1)}, u32[]{:S(2)}) copy-start(bf16[2,8192]{1,0:T(2,128)(2,1)} %param.13) | copy-start | bytes 98308
  23.8 7.3 %collective-permute-start = (bf16[640,128]{0,1:T(8,128)(2,1)S(1)}, bf16[640,128]{0,1:T(8,128)(2,1)S(1)}, u32[]{:S(2)}, u32[]{:S(2)}) collective-permute-start(bf16[640,128]{0,1:T(8,128)(2,1)S(1)} %pad_maximum_fusion.5), channel_id=1, source_target_pairs={{0,16},{16,0},{1,17},{17,1},{2,18},{18,2},{3,19},{19,3},{4,20},{20... | collective-permute-start | bytes 491528 | tf_op jit(solution)/shard_map/ppermute | solution.py:115
  26.8 9.1 %collective-permute-start.2 = (bf16[2,8192]{1,0:T(2,128)(2,1)S(1)}, bf16[2,8192]{1,0:T(2,128)(2,1)S(1)}, u32[]{:S(2)}, u32[]{:S(2)}) collective-permute-start(bf16[2,8192]{1,0:T(2,128)(2,1)S(1)} %copy-done.7), channel_id=1, source_target_pairs={{0,8},{1,9},{2,10},{3,11},{4,12},{5,13},{6,14},{7,15},{8,0},{9,1},... | collective-permute-start | bytes 98312 | tf_op jit(solution)/shard_map/ppermute | solution.py:117
  31.2 15.2 %collective-permute-start.1 = (bf16[640,256]{0,1:T(8,128)(2,1)S(1)}, bf16[640,256]{0,1:T(8,128)(2,1)S(1)}, u32[]{:S(2)}, u32[]{:S(2)}) collective-permute-start(bf16[640,256]{0,1:T(8,128)(2,1)S(1)} %pad_maximum_fusion.4), channel_id=1, source_target_pairs={{0,8},{1,9},{2,10},{3,11},{4,12},{5,13},{6,14},{7,15},{24,16},{25,... | collective-permute-start | bytes 983048 | tf_op jit(solution)/shard_map/ppermute | solution.py:120
  46.5 10.5 %collective-permute-start.3 = (bf16[1,768,256]{1,2,0:T(8,128)(2,1)S(1)}, bf16[1,768,256]{1,2,0:T(8,128)(2,1)S(1)}, u32[]{:S(2)}, u32[]{:S(2)}) collective-permute-start(bf16[1,768,256]{1,2,0:T(8,128)(2,1)S(1)} %maximum_bitcast_fusion), channel_id=1, source_target_pairs={{0,2},{1,3},{2,0},{3,1},{4,6},{5,7},{6,4},{7,5},{8,10},{9,11},{10,... | collective-permute-start | bytes 1179656 | tf_op jit(solution)/shard_map/ppermute | solution.py:125
  57.2 53.4 %collective-permute-start.4 = (bf16[2,768,256]{1,2,0:T(8,128)(2,1)S(1)}, bf16[2,768,256]{1,2,0:T(8,128)(2,1)}, u32[]{:S(2)}, u32[]{:S(2)}) collective-permute-start(bf16[2,768,256]{1,2,0:T(8,128)(2,1)S(1)} %pad_maximum_fusion.3), channel_id=1, source_target_pairs={{0,4},{1,5},{2,6},{3,7},{4,0},{5,1},{6,2},{7,3},{8,12},{9,13},{10,... | collective-permute-start | bytes 2359304 | tf_op jit(solution)/shard_map/ppermute | solution.py:125
  112.0 3.9 %collective-permute-start.5 = (bf16[4,768,256]{1,2,0:T(8,128)(2,1)S(1)}, bf16[4,768,256]{1,2,0:T(8,128)(2,1)}, u32[]{:S(2)}, u32[]{:S(2)}) collective-permute-start(bf16[4,768,256]{1,2,0:T(8,128)(2,1)S(1)} %pad_maximum_fusion.1), channel_id=1, source_target_pairs={{0,1},{1,0},{2,3},{3,2},{4,5},{5,4},{6,7},{7,6},{8,9},{9,8},{10,11... | collective-permute-start | bytes 4718600 | tf_op jit(solution)/shard_map/ppermute | solution.py:125
  112.7 4.7 %copy-start.8 = (s32[256]{0:T(256)}, s32[256]{0:T(256)S(1)}, u32[]{:S(2)}) copy-start(s32[256]{0:T(256)S(1)} %pad_add_fusion) | copy-start | bytes 3076
  122.9 0.6 copy-start.5
  124.2 25.0 %collective-permute-start.6 = (bf16[2,128,256]{1,2,0:T(8,128)(2,1)}, bf16[2,128,256]{1,2,0:T(8,128)(2,1)}, u32[]{:S(2)}, u32[]{:S(2)}) collective-permute-start(bf16[2,128,256]{1,2,0:T(8,128)(2,1)} %pad_maximum_fusion.6), channel_id=1, source_target_pairs={{0,16},{16,0},{1,17},{17,1},{2,18},{18,2},{3,19},{19,3},{4,20},{20... | collective-permute-start | bytes 393224 | tf_op jit(solution)/shard_map/ppermute | solution.py:150
  135.0 6.2 %copy-start.2 = (bf16[32,8192]{1,0:T(8,128)(2,1)S(1)}, bf16[32,8192]{1,0:T(8,128)(2,1)}, u32[]{:S(2)}) copy-start(bf16[32,8192]{1,0:T(8,128)(2,1)} %reshape.117) | copy-start | bytes 1572868
  141.3 4.7 %copy-start.1 = (f32[4096,256]{0,1:T(8,128)S(1)}, f32[4096,256]{0,1:T(8,128)}, u32[]{:S(2)}) copy-start(f32[4096,256]{0,1:T(8,128)} %copy.22) | copy-start | bytes 12582916
  141.3 4.7 %copy-start.9 = (s32[256]{0:T(256)S(1)}, s32[256]{0:T(256)}, u32[]{:S(2)}) copy-start(s32[256]{0:T(256)} %copy-done.8) | copy-start | bytes 3076
  146.0 3.0 %copy-start.10 = (s32[512]{0:T(512)S(1)}, s32[512]{0:T(512)}, u32[]{:S(2)}) copy-start(s32[512]{0:T(512)} %iota_add_fusion.1) | copy-start | bytes 6148
  146.0 3.3 %copy-start.6 = (bf16[1,128,256]{1,2,0:T(8,128)(2,1)S(1)}, bf16[1,128,256]{1,2,0:T(8,128)(2,1)}, u32[]{:S(2)}) copy-start(bf16[1,128,256]{1,2,0:T(8,128)(2,1)} %copy-done.5) | copy-start | bytes 196612
  149.3 54.1 %copy-start.4 = (f32[512,256]{0,1:T(8,128)}, f32[512,256]{0,1:T(8,128)S(1)}, u32[]{:S(2)}) copy-start(f32[512,256]{0,1:T(8,128)S(1)} %fusion.14) | copy-start | bytes 1572868
  198.0 5.3 %copy-start = (f32[256,4096]{1,0:T(8,128)S(1)}, f32[256,4096]{1,0:T(8,128)}, u32[]{:S(2)}) copy-start(f32[256,4096]{1,0:T(8,128)} %fusion.1) | copy-start | bytes 12582916
  198.9 10.3 %slice-start = ((s8[8388608]{0:T(1024)(128)(4,1)}), s8[4194304]{0:T(1024)(128)(4,1)S(1)}, s32[]{:S(2)}) async-start(s8[8388608]{0:T(1024)(128)(4,1)} %bitcast.62), calls=%async_computation.2 | async-start | bytes 8388608
  203.3 5.9 %slice-start.1 = ((s8[8388608]{0:T(1024)(128)(4,1)}), s8[4194304]{0:T(1024)(128)(4,1)S(1)}, s32[]{:S(2)}) async-start(s8[8388608]{0:T(1024)(128)(4,1)} %bitcast.62), calls=%async_computation.3 | async-start | bytes 8388608
  207.3 2.0 slice-start.2
  232.2 14.1 %collective-permute-start.7 = (bf16[512,512]{1,0:T(8,128)(2,1)S(1)}, bf16[512,512]{1,0:T(8,128)(2,1)S(1)}, u32[]{:S(2)}, u32[]{:S(2)}) collective-permute-start(bf16[512,512]{1,0:T(8,128)(2,1)S(1)} %dynamic-slice_convert_fusion.1), channel_id=1, source_target_pairs={{0,16},{16,0},{1,17},{17,1},{2,18},{18,2},{3,19},{19,3},{4,20},{20... | collective-permute-start | bytes 1572872 | tf_op jit(solution)/shard_map/ppermute | solution.py:179
  241.8 1.3 copy-start.3
  244.0 14.3 %collective-permute-start.8 = (bf16[512,512]{1,0:T(8,128)(2,1)}, bf16[512,512]{1,0:T(8,128)(2,1)}, u32[]{:S(2)}, u32[]{:S(2)}) collective-permute-start(bf16[512,512]{1,0:T(8,128)(2,1)} %dynamic-slice_convert_fusion), channel_id=1, source_target_pairs={{0,16},{16,0},{1,17},{17,1},{2,18},{18,2},{3,19},{19,3},{4,20},{20... | collective-permute-start | bytes 1572872 | tf_op jit(solution)/shard_map/ppermute | solution.py:179
Sparse Core Ops, SparseCore 0:
  10.1 98.4 all-gather.4
  110.8 79.0 all-gather.6
where the time goes:
time: 274 us; the launch traced here: 269 us
  waiting for transfers between devices  69.6 us (25%)
  other arithmetic  67.7 us (25%)
  matrix products  49.2 us (18%)
  starting transfers between devices  33.3 us (12%)
  local copies, waits for them, and re-layouts  33.3 us (12%)
  between operations  15.5 us (6%)
    ppermute x3, waiting for transfers between devices, on_device_pairs(): other = lax.ppermute(held, 'shard', [(i, i ^ bit) for i in range(shards)])  45.7 us
    another operation x6, other arithmetic, solve_spd(): lower_factor = jnp.linalg.cholesky(pivot_block)  25.1 us
    another operation x4, other arithmetic, solve_spd(): lax.linalg.triangular_solve(lower_factor, half_solved, left_side=True, lo...  21 us
    dot_general x2, matrix products, on_device_pairs(): lax.dot_general(half_swept, piece, (((1,), (1,)), ((), ())), preferred_el...  18.9 us
    ppermute x3, starting transfers between devices, on_device_pairs(): other = lax.ppermute(held, 'shard', [(i, i ^ bit) for i in range(shards)])  18.2 us
    unnamed x28, local copies, waits for them, and re-layouts  12.3 us
    ppermute x2, waiting for transfers between devices, on_device_pairs(): sent = lax.ppermute(theirs, 'group', swap)  12 us
    mul x2, local copies, waits for them, and re-layouts, damped(): ema_keep * old + (1.0 - ema_keep) * (cov / total)  11.7 us
  transfers between devices with their start and end apart: 11, of which 6 were waited for; matrix products, arithmetic and copies ran while one was open for 53% of the time, Pallas kernels for 0%

commit v1 on v0

--- a/solution.py
+++ b/solution.py
@@ -103,37 +103,44 @@
     bf16, f32 = jnp.bfloat16, jnp.float32
     half_count = shards // PIVOTS
     shard_half = shard // half_count
-    own = factor_old[:, :BLOCK]
+    own = lax.optimization_barrier(factor_old[:, :BLOCK]).T
     high = own.astype(bf16)
-    low = (own[:BLOCK] - high[:BLOCK].astype(f32)).astype(bf16)
+    low = (own[:, :BLOCK] - high[:, :BLOCK].astype(f32)).astype(bf16)
     swap = [(0, 1), (1, 0)]
 
     def ordered(first, mine, other, axis):
         return jnp.concatenate([jnp.where(first, mine, other), jnp.where(first, other, mine)], axis=axis)
 
-    mine = jnp.concatenate([high, low], axis=0)
-    pair = ordered(group == 0, mine, lax.ppermute(mine, "group", swap), 1)
     across = [(i, i ^ half_count) for i in range(shards)]
-    tokens = jnp.concatenate([samples, lax.ppermute(samples, "shard", across)], axis=0).reshape(-1, wide)
+    bits = [1 << k for k in range(half_count.bit_length() - 1)]
+    tops = jnp.stack([high[:, :BLOCK], low])
+    tops = ordered(group == 0, tops, lax.ppermute(tops, "group", swap), 1)
+    ends = [(i, j) for i, j in across if i % half_count == 0]
+    tops = ordered(shard_half == 0, tops, lax.ppermute(tops, "shard", ends), 2)
+    tokens = jnp.concatenate([samples, lax.ppermute(samples, "shard", across)], axis=0)
+    for bit in bits[::-1]:
+        tree = [(i, i ^ bit) for i in range(shards) if i % (2 * bit) == 0]
+        tops = jnp.where(shard % (2 * bit) == bit, lax.ppermute(tops, "shard", tree), tops)
+        other = lax.ppermute(tokens, "shard", [(i, i ^ bit) for i in range(shards)])
+        tokens = jnp.concatenate([tokens, other], axis=0)
+    tops = tops.astype(f32)
+    pair = ordered(group == 0, high, lax.ppermute(high, "group", swap), 0)
     one_way = [(g * shards + i, g * shards + (i ^ half_count))
                for g in range(PIVOTS) for i in range(shards) if i // half_count == g]
     moved = lax.ppermute(pair, ("group", "shard"), one_way)
-    held = jnp.concatenate([jnp.where(shard_half == group, pair, moved), tokens], axis=0)[None]
-    bits = [1 << k for k in range(half_count.bit_length() - 1)]
-    bits = bits[1:] + bits[:1]
-    for bit in bits:
+    held = jnp.where(shard_half == group, pair, moved)
+    for bit in bits[1:]:
         other = lax.ppermute(held, "shard", [(i, i ^ bit) for i in range(shards)])
-        held = ordered((shard & bit) == 0, held, other, 0)
-    depth = held.shape[1]
-    held = jnp.swapaxes(held.reshape(2, half_count // 2, depth, wide), 0, 1)
-    held = held.reshape(half_count, depth, wide)
+        held = ordered((shard & bit) == 0, held, other, 1)
+    other = lax.ppermute(held, "shard", [(i, i ^ 1) for i in range(shards)])
+    even, odd = jnp.where(shard % 2 == 0, held, other), jnp.where(shard % 2 == 0, other, held)
+    strip = jnp.concatenate([piece[:, i:i + rows] for i in range(0, even.shape[1], rows)
+                             for piece in (even, odd)], axis=1).astype(f32)
     units = gradients.shape[0] // 2
     gathered = []
     for half in range(2):
         piece = gradients[half * units:(half + 1) * units]
         gathered.append(lax.all_gather(piece, "shard", axis=0, tiled=False))
-    tokens = held[:, rows + BLOCK:].reshape(total, D)
-    columns = held[:, :rows].reshape(cols, wide)
     spacing = D // PIVOTS
     ptok = jnp.concatenate([tokens[:, p * spacing:p * spacing + BLOCK] for p in range(PIVOTS)], axis=1)
     pidx = jnp.concatenate([jnp.arange(BLOCK) + p * spacing for p in range(PIVOTS)])
@@ -142,12 +149,9 @@
     rid = jnp.arange(rows) + row_first
     cid = jnp.arange(cols) + col_first
     d0 = damping[0]
-    col_own = pair[:rows].astype(f32)
+    col_own = pair.T.astype(f32)
     C = damped(col_own, left, ptok, total, rid[:, None] == pidx[None, :], d0)
-    strip = columns.T.astype(f32)
     R = damped(strip, ptok, right, total, pidx[:, None] == cid[None, :], d0)
-    tops = jnp.stack([held[0, :BLOCK], held[0, rows:rows + BLOCK]])
-    tops = ordered(group == 0, tops, lax.ppermute(tops, "group", swap), 1).astype(f32)
     A = damped(tops[0] + tops[1], ptok, ptok, total, pidx[:, None] == pidx[None, :], d0)
     E = jnp.where(pidx[:, None] == cid[None, :], 1.0, 0.0).astype(f32)
     ones = jnp.eye(BLOCK, dtype=f32)

time: 274 us -> 222 us (0.81)
  local copies, waits for them, and re-layouts: 33.3 us -> 10.9 us
  waiting for transfers between devices: 69.6 us -> 55.4 us
  other arithmetic: 67.7 us -> 57.4 us
  matrix products: 49.2 us -> 40 us
  starting transfers between devices: 33.3 us -> 39.1 us
    ppermute x3 -> x2, waiting for transfers between devices: 45.7 us -> 0.01 us  [on_device_pairs(): other = lax.ppermute(held, 'shard', [(i, i ^ bit) for i in range(shards)])]
    all_gather x2, waiting for transfers between devices: 0.02 us -> 20.5 us  [on_device_pairs(): gathered.append(lax.all_gather(piece, 'shard', axis=0, tiled=False))]
    ppermute x2 -> x10, waiting for transfers between devices: 1.65 us -> 19.1 us  [the longest x3 9.54 us: on_device_pairs(): lax.ppermute(tops, 'shard', tree)]
    mul x2 -> x0, local copies, waits for them, and re-layouts: 11.7 us -> none  [damped(): ema_keep * old + (1.0 - ema_keep) * (cov / total)]
    ppermute x2 -> x10, starting transfers between devices: 5.75 us -> 13.3 us  [the longest x3 4.09 us: on_device_pairs(): lax.ppermute(tops, 'shard', tree)]
    unnamed x28 -> x42, local copies, waits for them, and re-layouts: 12.3 us -> 5.07 us
    ppermute x1, waiting for transfers between devices: 10.2 us -> 3.13 us  [on_device_pairs(): moved = lax.ppermute(pair, ('group', 'shard'), one_way)]
    ppermute x2, starting transfers between devices: 2.02 us -> 8.13 us  [on_device_pairs(): sent = lax.ppermute(theirs, 'group', swap)]
  transfers between devices with their start and end apart: 11 -> 18, of which waited for: 6 -> 7; matrix products, arithmetic and copies ran while one was open for 53% -> 45% of each run, Pallas kernels for 0% -> 0%
where the time goes in v1:
time: 222 us; the launch traced here: 219 us
  other arithmetic  57.4 us (26%)
  waiting for transfers between devices  55.4 us (25%)
  matrix products  40 us (18%)
  starting transfers between devices  39.1 us (18%)
  between operations  15.9 us (7%)
  local copies, waits for them, and re-layouts  10.9 us (5%)
    another operation x6, other arithmetic, solve_spd(): lower_factor = jnp.linalg.cholesky(pivot_block)  24.8 us
    another operation x4, other arithmetic, solve_spd(): lax.linalg.triangular_solve(lower_factor, half_solved, left_side=True, lo...  21.2 us
    all_gather x2, waiting for transfers between devices, on_device_pairs(): gathered.append(lax.all_gather(piece, 'shard', axis=0, tiled=False))  20.5 us
    dot_general x2, matrix products, on_device_pairs(): lax.dot_general(half_swept, piece, (((1,), (1,)), ((), ())), preferred_el...  18.9 us
    ppermute x2, starting transfers between devices, on_device_pairs(): other = lax.ppermute(held, 'shard', [(i, i ^ bit) for i in range(shards)])  13.8 us
    ppermute x2, waiting for transfers between devices, on_device_pairs(): sent = lax.ppermute(theirs, 'group', swap)  12.6 us
    ppermute x3, waiting for transfers between devices, on_device_pairs(): lax.ppermute(tops, 'shard', tree)  9.54 us
    dot_general x6, matrix products, exact(): jnp.dot(a, b, precision=lax.Precision.HIGHEST, preferred_element_type=jnp...  9.31 us
  transfers between devices with their start and end apart: 18, of which 7 were waited for; matrix products, arithmetic and copies ran while one was open for 45% of the time, Pallas kernels for 0%

profile of v1, /device:TPU:0, one launch (start us, length us, event | category | flops | bytes accessed | tf_op | source)
XLA Modules:
  0.0 218.8 jit_solution(17941978608891891104)
XLA Ops:
  7.2 2.3 %fusion.58 = (bf16[64,4096]{1,0:T(8,128)(2,1)}, bf16[64,4096]{1,0:T(8,128)(2,1)}) fusion(bf16[128,4096]{1,0:T(8,128)(2,1)} %param.16), kind=kLoop, calls=%fused_computation.125 | loop fusion | bytes 2097152 | tf_op jit(solution)/shard_map/slice | solution.py:142
  10.5 3.1 %collective-permute-start.4 = (bf16[128,512]{0,1:T(8,128)(2,1)S(1)}, bf16[128,512]{0,1:T(8,128)(2,1)S(1)}, u32[]{:S(2)}, u32[]{:S(2)}) collective-permute-start(bf16[128,512]{0,1:T(8,128)(2,1)S(1)} %bitcast_convert_fusion), channel_id=1, source_target_pairs={{0,16},{16,0},{1,17},{17,1},{2,18},{18,2},{3,19},{19,3},{4,20},{20... | collective-permute-start | bytes 393224 | tf_op jit(solution)/shard_map/ppermute | solution.py:127
  13.6 2.6 %collective-permute-start = (bf16[2,8192]{1,0:T(2,128)(2,1)S(1)}, bf16[2,8192]{1,0:T(2,128)(2,1)S(1)}, u32[]{:S(2)}, u32[]{:S(2)}) collective-permute-start(bf16[2,8192]{1,0:T(2,128)(2,1)S(1)} %copy-done.3), channel_id=1, source_target_pairs={{0,8},{1,9},{2,10},{3,11},{4,12},{5,13},{6,14},{7,15},{8,0},{9,1},... | collective-permute-start | bytes 98312 | tf_op jit(solution)/shard_map/ppermute | solution.py:120
  16.9 3.4 %compare_select_fusion = f32[256,4096]{0,1:T(8,128)} fusion(s32[256]{0:T(256)S(1)} %pad_add_fusion, s32[4096]{0:T(1024)S(1)} %iota_add_fusion), kind=kLoop, calls=%fused_computation.2 | loop fusion | flops 2097152 | bytes 4211712 | tf_op jit(solution)/shard_map/jit(_where)/select_n | solution.py:156
  21.1 1.6 collective-permute-start.1
  22.8 2.2 %collective-permute-start.6 = (bf16[2,256,128]{1,2,0:T(8,128)(2,1)S(1)}, bf16[2,256,128]{1,2,0:T(8,128)(2,1)S(1)}, u32[]{:S(2)}, u32[]{:S(2)}) collective-permute-start(bf16[2,256,128]{1,2,0:T(8,128)(2,1)S(1)} %pad_maximum_fusion.7), channel_id=1, source_target_pairs={{0,8},{8,0},{16,24},{24,16}} | collective-permute-start | bytes 393224 | tf_op jit(solution)/shard_map/ppermute | solution.py:119
  25.0 3.6 %collective-permute-done.1 = bf16[4,8192]{1,0:T(4,128)(2,1)S(1)} collective-permute-done((bf16[4,8192]{1,0:T(4,128)(2,1)S(1)}, bf16[4,8192]{1,0:T(4,128)(2,1)S(1)}, u32[]{:S(2)}, u32[]{:S(2)}) %collective-permute-start.1) | collective-permute-done | bytes 65568 | tf_op jit(solution)/shard_map/ppermute | solution.py:124
  28.8 1.6 collective-permute-start.2
  31.7 5.9 %collective-permute-done.6 = bf16[2,256,128]{1,2,0:T(8,128)(2,1)S(1)} collective-permute-done((bf16[2,256,128]{1,2,0:T(8,128)(2,1)S(1)}, bf16[2,256,128]{1,2,0:T(8,128)(2,1)S(1)}, u32[]{:S(2)}, u32[]{:S(2)}) %collective-permute-start.6) | collective-permute-done | bytes 131104 | tf_op jit(solution)/shard_map/ppermute | solution.py:119
  39.3 3.1 %collective-permute-done.10 = bf16[256,512]{0,1:T(8,128)(2,1)S(1)} collective-permute-done((bf16[256,512]{0,1:T(8,128)(2,1)S(1)}, bf16[256,512]{0,1:T(8,128)(2,1)S(1)}, u32[]{:S(2)}, u32[]{:S(2)}) %collective-permute-start.10) | collective-permute-done | bytes 262176 | tf_op jit(solution)/shard_map/ppermute | solution.py:130
  42.8 7.1 %collective-permute-done.7 = bf16[2,256,256]{1,2,0:T(8,128)(2,1)S(1)} collective-permute-done((bf16[2,256,256]{1,2,0:T(8,128)(2,1)S(1)}, bf16[2,256,256]{1,2,0:T(8,128)(2,1)S(1)}, u32[]{:S(2)}, u32[]{:S(2)}) %collective-permute-start.7) | collective-permute-done | bytes 262176 | tf_op jit(solution)/shard_map/ppermute | solution.py:123
  52.6 2.5 %collective-permute-done.8 = bf16[2,256,256]{1,2,0:T(8,128)(2,1)S(1)} collective-permute-done((bf16[2,256,256]{1,2,0:T(8,128)(2,1)S(1)}, bf16[2,256,256]{1,2,0:T(8,128)(2,1)S(1)}, u32[]{:S(2)}, u32[]{:S(2)}) %collective-permute-start.8) | collective-permute-done | bytes 262176 | tf_op jit(solution)/shard_map/ppermute | solution.py:123
  55.2 1.5 collective-permute-start.9
  56.7 13.5 %collective-permute-start.12 = (bf16[256,1024]{0,1:T(8,128)(2,1)S(1)}, bf16[256,1024]{0,1:T(8,128)(2,1)S(1)}, u32[]{:S(2)}, u32[]{:S(2)}) collective-permute-start(bf16[256,1024]{0,1:T(8,128)(2,1)S(1)} %pad_maximum_fusion.2), channel_id=1, source_target_pairs={{0,4},{1,5},{2,6},{3,7},{4,0},{5,1},{6,2},{7,3},{8,12},{9,13},{10,... | collective-permute-start | bytes 1572872 | tf_op jit(solution)/shard_map/ppermute | solution.py:133
  70.7 11.7 %cholesky.44 = f32[128,128]{1,0:T(8,128)S(1)} custom-call(f32[128,128]{1,0:T(8,128)S(1)} %fusion.41), custom_call_target="Cholesky" | custom-call | tf_op jit(solution)/shard_map/jit(cholesky)/cholesky | solution.py:20
  83.8 9.8 %custom-call.11 = f32[1,128,128]{1,2,0:T(8,128)S(1)} custom-call(f32[1,128,128]{2,1,0:T(8,128)S(1)} %fusion.28), custom_call_target="InvertDiagBlocksLowerTriangular" | custom-call | tf_op jit(solution)/shard_map/triangular_solve/custom-call.2 | solution.py:22
  95.4 11.7 %cholesky.55 = f32[128,128]{1,0:T(8,128)S(1)} custom-call(f32[128,128]{1,0:T(8,128)S(1)} %fusion.37), custom_call_target="Cholesky" | custom-call | tf_op jit(solution)/shard_map/jit(cholesky)/cholesky | solution.py:20
  109.8 10.0 %custom-call.13 = f32[1,128,128]{1,2,0:T(8,128)S(1)} custom-call(f32[1,128,128]{2,1,0:T(8,128)S(1)} %fusion.29), custom_call_target="InvertDiagBlocksLowerTriangular" | custom-call | tf_op jit(solution)/shard_map/triangular_solve/custom-call.2 | solution.py:22
  120.3 1.4 slice_subtract_fusion
  125.1 1.9 fusion.7
  127.0 3.6 %fusion = f32[128,4096]{0,1:T(8,128)S(1)} fusion(f32[128,4096]{1,0:T(8,128)S(1)} %fusion.7, f32[256,4096]{0,1:T(8,128)S(1)} %copy-done, f32[256,4096]{0,1:T(8,128)S(1)} %fusion.1, f32[256,256]{0,1:T(8,128)S(1)} %fusion.16), kind=kOutput, calls=%fused_computation.5 | convolution fusion | flops 806354944 | bytes 8454144 | tf_op jit(solution)/shard_map/dot_general | solution.py:92
  130.6 2.0 fusion.60
  132.6 4.2 %fusion.2 = f32[512,4096]{1,0:T(8,128)S(1)} fusion(f32[128,4096]{1,0:T(8,128)S(1)} %fusion.60, f32[128,4096]{1,0:T(8,128)S(1)} %fusion.7, f32[512,128]{1,0:T(8,128)S(1)} %fusion.30, f32[512,128]{1,0:T(8,128)S(1)} %slice-done.2), kind=kOutput, calls=%fused_computation.7 | convolution fusion | flops 3222405120 | bytes 13107200 | tf_op jit(solution)/shard_map/dot_general | solution.py:172
  136.9 4.8 %add_subtract_fusion = f32[512,4096]{1,0:T(8,128)} fusion(f32[512,4096]{1,0:T(8,128)S(1)} %fusion.2, f32[512,4096]{1,0:T(8,128)S(1)} %bitcast.60, f32[]{:T(128)} %bitcast.55, s32[4096]{0:T(1024)S(1)} %iota_add_fusion, s32[512]{0:T(512)S(1)} %copy-done.12, bf16[32,8192]{1,0:T(8,128)(2,1)S(1)} %concatenate.55, s32[]{:T(128)S(6)} %select_n.183, s32[]{:T(128)S(6)} %select_n.182), kind=kOutput, calls=%fused_computation | convolution fusion | flops 148897792 | bytes 25479180 | tf_op jit(solution)/shard_map/dot_general | solution.py:87
  141.6 3.7 %fusion.6 = f32[512,4096]{1,0:T(8,128)} fusion(f32[512,4096]{1,0:T(8,128)} %add_subtract_fusion, f32[128,4096]{1,0:T(8,128)S(1)} %fusion.7, f32[128,4096]{1,0:T(8,128)S(1)} %fusion.60, pred[]{:T(512)S(6)} %eq.128, pred[]{:T(512)S(6)} %eq.120), kind=kLoop, calls=%fused_computation.12 | loop fusion | flops 1572864 | bytes 8388610 | tf_op jit(solution)/shard_map/scatter-add | solution.py:175
  145.4 9.5 %fusion.11 = f32[512,1024]{1,0:T(8,128)S(1)} fusion(bf16[1024,4096]{1,0:T(8,128)(2,1)} %all-gather.5.cloned.1.call-done, f32[512,4096]{1,0:T(8,128)} %fusion.6), kind=kOutput, calls=%fused_computation.18 | convolution fusion | flops 4297064448 | bytes 18874368 | tf_op jit(solution)/shard_map/dot_general | solution.py:181
  155.0 6.7 %collective-permute-start.14 = (bf16[512,512]{1,0:T(8,128)(2,1)S(1)}, bf16[512,512]{1,0:T(8,128)(2,1)S(1)}, u32[]{:S(2)}, u32[]{:S(2)}) collective-permute-start(bf16[512,512]{1,0:T(8,128)(2,1)S(1)} %dynamic-slice_convert_fusion.1), channel_id=1, source_target_pairs={{0,16},{16,0},{1,17},{17,1},{2,18},{18,2},{3,19},{19,3},{4,20},{20... | collective-permute-start | bytes 1572872 | tf_op jit(solution)/shard_map/ppermute | solution.py:183
  161.6 20.5 %all-gather.7.cloned.1.call-done = bf16[1024,4096]{1,0:T(8,128)(2,1)} async-done(((bf16[64,4096]{1,0:T(8,128)(2,1)}), bf16[1024,4096]{1,0:T(8,128)(2,1)}) %all-gather.7.cloned.1.call-update) | async-done | bytes 8388624 | tf_op jit(solution)/shard_map/all_gather | solution.py:143
  182.2 9.4 %fusion.9 = f32[512,1024]{1,0:T(8,128)S(1)} fusion(bf16[1024,4096]{1,0:T(8,128)(2,1)} %all-gather.7.cloned.1.call-done, f32[512,4096]{1,0:T(8,128)} %fusion.6), kind=kOutput, calls=%fused_computation.16 | convolution fusion | flops 4297064448 | bytes 18874368 | tf_op jit(solution)/shard_map/dot_general | solution.py:181
  193.8 1.5 collective-permute-start.15
  195.7 12.5 %collective-permute-done.15 = bf16[512,512]{1,0:T(8,128)(2,1)} collective-permute-done((bf16[512,512]{1,0:T(8,128)(2,1)}, bf16[512,512]{1,0:T(8,128)(2,1)}, u32[]{:S(2)}, u32[]{:S(2)}) %collective-permute-start.15) | collective-permute-done | bytes 524320 | tf_op jit(solution)/shard_map/ppermute | solution.py:183
  208.2 1.6 add_convert_fusion
  (127 shorter events, 22.4 us)
Async XLA Ops:
  7.2 6.4 %copy-start.3 = (bf16[2,8192]{1,0:T(2,128)(2,1)S(1)}, bf16[2,8192]{1,0:T(2,128)(2,1)}, u32[]{:S(2)}) copy-start(bf16[2,8192]{1,0:T(2,128)(2,1)} %param.13) | copy-start | bytes 98308
  7.2 138.2 %all-gather.5.cloned.1.call-start = ((), (), s32[]{:S(2)}) async-start(), calls=%async_computation | async-start | bytes 8912896 | tf_op jit(solution)/shard_map/all_gather | solution.py:143
  9.5 172.7 %all-gather.7.cloned.1.call-start = ((), (), s32[]{:S(2)}) async-start(), calls=%async_computation.1 | async-start | bytes 8912896 | tf_op jit(solution)/shard_map/all_gather | solution.py:143
  10.5 19.8 %collective-permute-start.4 = (bf16[128,512]{0,1:T(8,128)(2,1)S(1)}, bf16[128,512]{0,1:T(8,128)(2,1)S(1)}, u32[]{:S(2)}, u32[]{:S(2)}) collective-permute-start(bf16[128,512]{0,1:T(8,128)(2,1)S(1)} %bitcast_convert_fusion), channel_id=1, source_target_pairs={{0,16},{16,0},{1,17},{17,1},{2,18},{18,2},{3,19},{19,3},{4,20},{20... | collective-permute-start | bytes 393224 | tf_op jit(solution)/shard_map/ppermute | solution.py:127
  13.6 7.4 %collective-permute-start = (bf16[2,8192]{1,0:T(2,128)(2,1)S(1)}, bf16[2,8192]{1,0:T(2,128)(2,1)S(1)}, u32[]{:S(2)}, u32[]{:S(2)}) collective-permute-start(bf16[2,8192]{1,0:T(2,128)(2,1)S(1)} %copy-done.3), channel_id=1, source_target_pairs={{0,8},{1,9},{2,10},{3,11},{4,12},{5,13},{6,14},{7,15},{8,0},{9,1},... | collective-permute-start | bytes 98312 | tf_op jit(solution)/shard_map/ppermute | solution.py:120
  16.2 6.5 %collective-permute-start.5 = (bf16[2,128,128]{1,2,0:T(8,128)(2,1)S(1)}, bf16[2,128,128]{1,2,0:T(8,128)(2,1)S(1)}, u32[]{:S(2)}, u32[]{:S(2)}) collective-permute-start(bf16[2,128,128]{1,2,0:T(8,128)(2,1)S(1)} %pad_maximum_fusion.9), channel_id=1, source_target_pairs={{0,16},{16,0},{1,17},{17,1},{2,18},{18,2},{3,19},{19,3},{4,20},{20... | collective-permute-start | bytes 196616 | tf_op jit(solution)/shard_map/ppermute | solution.py:117
  16.9 53.4 %copy-start.13 = (s32[256]{0:T(256)}, s32[256]{0:T(256)S(1)}, u32[]{:S(2)}) copy-start(s32[256]{0:T(256)S(1)} %pad_add_fusion) | copy-start | bytes 3076
  20.3 31.3 %copy-start.11 = (s32[512]{0:T(512)}, s32[512]{0:T(512)S(1)}, u32[]{:S(2)}) copy-start(s32[512]{0:T(512)S(1)} %iota_add_fusion.1) | copy-start | bytes 6148
  21.1 7.6 %collective-permute-start.1 = (bf16[4,8192]{1,0:T(4,128)(2,1)S(1)}, bf16[4,8192]{1,0:T(4,128)(2,1)S(1)}, u32[]{:S(2)}, u32[]{:S(2)}) collective-permute-start(bf16[4,8192]{1,0:T(4,128)(2,1)S(1)} %pad_maximum_fusion.8), channel_id=1, source_target_pairs={{0,4},{1,5},{2,6},{3,7},{4,0},{5,1},{6,2},{7,3},{8,12},{9,13},{10,... | collective-permute-start | bytes 196616 | tf_op jit(solution)/shard_map/ppermute | solution.py:124
  22.8 14.9 %collective-permute-start.6 = (bf16[2,256,128]{1,2,0:T(8,128)(2,1)S(1)}, bf16[2,256,128]{1,2,0:T(8,128)(2,1)S(1)}, u32[]{:S(2)}, u32[]{:S(2)}) collective-permute-start(bf16[2,256,128]{1,2,0:T(8,128)(2,1)S(1)} %pad_maximum_fusion.7), channel_id=1, source_target_pairs={{0,8},{8,0},{16,24},{24,16}} | collective-permute-start | bytes 393224 | tf_op jit(solution)/shard_map/ppermute | solution.py:119
  28.8 10.3 %collective-permute-start.2 = (bf16[8,8192]{1,0:T(8,128)(2,1)S(1)}, bf16[8,8192]{1,0:T(8,128)(2,1)S(1)}, u32[]{:S(2)}, u32[]{:S(2)}) collective-permute-start(bf16[8,8192]{1,0:T(8,128)(2,1)S(1)} %pad_maximum_fusion.6), channel_id=1, source_target_pairs={{0,2},{1,3},{2,0},{3,1},{4,6},{5,7},{6,4},{7,5},{8,10},{9,11},{10,... | collective-permute-start | bytes 393224 | tf_op jit(solution)/shard_map/ppermute | solution.py:124
  30.4 12.1 %collective-permute-start.10 = (bf16[256,512]{0,1:T(8,128)(2,1)S(1)}, bf16[256,512]{0,1:T(8,128)(2,1)S(1)}, u32[]{:S(2)}, u32[]{:S(2)}) collective-permute-start(bf16[256,512]{0,1:T(8,128)(2,1)S(1)} %pad_maximum_fusion.4), channel_id=1, source_target_pairs={{0,8},{1,9},{2,10},{3,11},{4,12},{5,13},{6,14},{7,15},{24,16},{25,... | collective-permute-start | bytes 786440 | tf_op jit(solution)/shard_map/ppermute | solution.py:130
  37.7 12.1 %collective-permute-start.7 = (bf16[2,256,256]{1,2,0:T(8,128)(2,1)S(1)}, bf16[2,256,256]{1,2,0:T(8,128)(2,1)S(1)}, u32[]{:S(2)}, u32[]{:S(2)}) collective-permute-start(bf16[2,256,256]{1,2,0:T(8,128)(2,1)S(1)} %pad_maximum_fusion.5), channel_id=1, source_target_pairs={{0,4},{8,12},{16,20},{24,28}} | collective-permute-start | bytes 786440 | tf_op jit(solution)/shard_map/ppermute | solution.py:123
  39.3 12.0 %collective-permute-start.3 = (bf16[16,8192]{1,0:T(8,128)(2,1)S(1)}, bf16[16,8192]{1,0:T(8,128)(2,1)S(1)}, u32[]{:S(2)}, u32[]{:S(2)}) collective-permute-start(bf16[16,8192]{1,0:T(8,128)(2,1)S(1)} %pad_maximum_fusion.3), channel_id=1, source_target_pairs={{0,1},{1,0},{2,3},{3,2},{4,5},{5,4},{6,7},{7,6},{8,9},{9,8},{10,11... | collective-permute-start | bytes 786440 | tf_op jit(solution)/shard_map/ppermute | solution.py:124
  42.5 14.1 %collective-permute-start.11 = (bf16[256,512]{0,1:T(8,128)(2,1)S(1)}, bf16[256,512]{0,1:T(8,128)(2,1)S(1)}, u32[]{:S(2)}, u32[]{:S(2)}) collective-permute-start(bf16[256,512]{0,1:T(8,128)(2,1)S(1)} %broadcast_select_fusion.4), channel_id=1, source_target_pairs={{0,2},{1,3},{2,0},{3,1},{4,6},{5,7},{6,4},{7,5},{8,10},{9,11},{10,... | collective-permute-start | bytes 786440 | tf_op jit(solution)/shard_map/ppermute | solution.py:133
  50.0 5.2 %collective-permute-start.8 = (bf16[2,256,256]{1,2,0:T(8,128)(2,1)S(1)}, bf16[2,256,256]{1,2,0:T(8,128)(2,1)S(1)}, u32[]{:S(2)}, u32[]{:S(2)}) collective-permute-start(bf16[2,256,256]{1,2,0:T(8,128)(2,1)S(1)} %broadcast_select_fusion.7), channel_id=1, source_target_pairs={{0,2},{4,6},{8,10},{12,14},{16,18},{20,22},{24,26},{28,30}} | collective-permute-start | bytes 786440 | tf_op jit(solution)/shard_map/ppermute | solution.py:123
  51.5 18.8 %copy-start.7 = (bf16[32,128]{1,0:T(8,128)(2,1)}, bf16[32,128]{1,0:T(8,128)(2,1)S(1)}, u32[]{:S(2)}) copy-start(bf16[32,128]{1,0:T(8,128)(2,1)S(1)} %get-tuple-element.39) | copy-start | bytes 24580
  51.5 18.8 %copy-start.9 = (bf16[32,128]{1,0:T(8,128)(2,1)}, bf16[32,128]{1,0:T(8,128)(2,1)S(1)}, u32[]{:S(2)}) copy-start(bf16[32,128]{1,0:T(8,128)(2,1)S(1)} %get-tuple-element.40) | copy-start | bytes 24580
  51.8 0.8 copy-start.2
  55.2 15.1 %collective-permute-start.9 = (bf16[2,256,256]{1,2,0:T(8,128)(2,1)S(1)}, bf16[2,256,256]{1,2,0:T(8,128)(2,1)S(1)}, u32[]{:S(2)}, u32[]{:S(2)}) collective-permute-start(bf16[2,256,256]{1,2,0:T(8,128)(2,1)S(1)} %broadcast_select_fusion.8), channel_id=1, source_target_pairs={{0,1},{2,3},{4,5},{6,7},{8,9},{10,11},{12,13},{14,15},{16,17},{18,... | collective-permute-start | bytes 786440 | tf_op jit(solution)/shard_map/ppermute | solution.py:123
  56.7 51.1 %collective-permute-start.12 = (bf16[256,1024]{0,1:T(8,128)(2,1)S(1)}, bf16[256,1024]{0,1:T(8,128)(2,1)S(1)}, u32[]{:S(2)}, u32[]{:S(2)}) collective-permute-start(bf16[256,1024]{0,1:T(8,128)(2,1)S(1)} %pad_maximum_fusion.2), channel_id=1, source_target_pairs={{0,4},{1,5},{2,6},{3,7},{4,0},{5,1},{6,2},{7,3},{8,12},{9,13},{10,... | collective-permute-start | bytes 1572872 | tf_op jit(solution)/shard_map/ppermute | solution.py:133
  107.9 1.2 copy-start.6
  108.1 13.7 %copy-start.4 = (f32[128,128]{1,0:T(8,128)S(1)}, f32[128,128]{1,0:T(8,128)}, u32[]{:S(2)}) copy-start(f32[128,128]{1,0:T(8,128)} %copy.19) | copy-start | bytes 196612
  109.1 12.7 %collective-permute-start.13 = (bf16[256,2048]{0,1:T(8,128)(2,1)}, bf16[256,2048]{0,1:T(8,128)(2,1)S(1)}, u32[]{:S(2)}, u32[]{:S(2)}) collective-permute-start(bf16[256,2048]{0,1:T(8,128)(2,1)} %pad_maximum_fusion), channel_id=1, source_target_pairs={{0,1},{1,0},{2,3},{3,2},{4,5},{5,4},{6,7},{7,6},{8,9},{9,8},{10,11... | collective-permute-start | bytes 3145736 | tf_op jit(solution)/shard_map/ppermute | solution.py:135
  122.9 2.2 %copy-start = (f32[256,4096]{0,1:T(8,128)S(1)}, f32[256,4096]{0,1:T(8,128)}, u32[]{:S(2)}) copy-start(f32[256,4096]{0,1:T(8,128)} %compare_select_fusion) | copy-start | bytes 12582916
  126.9 5.6 %slice-start.2 = ((f32[512,256]{1,0:T(8,128)}), f32[512,128]{1,0:T(8,128)S(1)}, s32[]{:S(2)}) async-start(f32[512,256]{1,0:T(8,128)} %copy-done.2), calls=%async_computation.4 | async-start | bytes 524288 | tf_op jit(solution)/shard_map/slice | solution.py:170
  130.6 6.2 %slice-start = ((s8[8388608]{0:T(1024)(128)(4,1)}), s8[4194304]{0:T(1024)(128)(4,1)S(1)}, s32[]{:S(2)}) async-start(s8[8388608]{0:T(1024)(128)(4,1)} %bitcast.59), calls=%async_computation.2 | async-start | bytes 8388608
  132.6 4.2 %slice-start.1 = ((s8[8388608]{0:T(1024)(128)(4,1)}), s8[4194304]{0:T(1024)(128)(4,1)S(1)}, s32[]{:S(2)}) async-start(s8[8388608]{0:T(1024)(128)(4,1)} %bitcast.59), calls=%async_computation.3 | async-start | bytes 8388608
  132.6 4.2 %copy-start.12 = (s32[512]{0:T(512)S(1)}, s32[512]{0:T(512)}, u32[]{:S(2)}) copy-start(s32[512]{0:T(512)} %copy-done.11) | copy-start | bytes 6148
  155.0 40.3 %collective-permute-start.14 = (bf16[512,512]{1,0:T(8,128)(2,1)S(1)}, bf16[512,512]{1,0:T(8,128)(2,1)S(1)}, u32[]{:S(2)}, u32[]{:S(2)}) collective-permute-start(bf16[512,512]{1,0:T(8,128)(2,1)S(1)} %dynamic-slice_convert_fusion.1), channel_id=1, source_target_pairs={{0,16},{16,0},{1,17},{17,1},{2,18},{18,2},{3,19},{19,3},{4,20},{20... | collective-permute-start | bytes 1572872 | tf_op jit(solution)/shard_map/ppermute | solution.py:183
  191.6 1.4 copy-start.1
  193.8 14.4 %collective-permute-start.15 = (bf16[512,512]{1,0:T(8,128)(2,1)}, bf16[512,512]{1,0:T(8,128)(2,1)}, u32[]{:S(2)}, u32[]{:S(2)}) collective-permute-start(bf16[512,512]{1,0:T(8,128)(2,1)} %dynamic-slice_convert_fusion), channel_id=1, source_target_pairs={{0,16},{16,0},{1,17},{17,1},{2,18},{18,2},{3,19},{19,3},{4,20},{20... | collective-permute-start | bytes 1572872 | tf_op jit(solution)/shard_map/ppermute | solution.py:183
  (4 other events, 2.9 us)
Sparse Core Ops, SparseCore 0:
  10.1 95.3 all-gather.4
  107.7 74.4 all-gather.6

commit v2 on v1

--- a/solution.py
+++ b/solution.py
@@ -136,11 +136,9 @@
     even, odd = jnp.where(shard % 2 == 0, held, other), jnp.where(shard % 2 == 0, other, held)
     strip = jnp.concatenate([piece[:, i:i + rows] for i in range(0, even.shape[1], rows)
                              for piece in (even, odd)], axis=1).astype(f32)
-    units = gradients.shape[0] // 2
-    gathered = []
-    for half in range(2):
-        piece = gradients[half * units:(half + 1) * units]
-        gathered.append(lax.all_gather(piece, "shard", axis=0, tiled=False))
+    most = gradients.shape[0] * 3 // 4
+    gathered = [lax.all_gather(piece, "shard", axis=0, tiled=False)
+                for piece in (gradients[:most], gradients[most:])]
     spacing = D // PIVOTS
     ptok = jnp.concatenate([tokens[:, p * spacing:p * spacing + BLOCK] for p in range(PIVOTS)], axis=1)
     pidx = jnp.concatenate([jnp.arange(BLOCK) + p * spacing for p in range(PIVOTS)])
@@ -182,7 +180,7 @@
         theirs = lax.dynamic_slice_in_dim(part, (1 - group) * width, width, 1).astype(bf16)
         sent = lax.ppermute(theirs, "group", swap)
         ours = lax.dynamic_slice_in_dim(part, group * width, width, 1)
-        out.append((ours + sent.astype(f32)).astype(bf16).reshape(rows, half_count, 1, units))
+        out.append((ours + sent.astype(f32)).astype(bf16).reshape(rows, half_count, -1))
     update = jnp.concatenate(out, axis=2).reshape(rows, -1)
     return (swept, update)
 

time: 222 us -> 212 us (0.955)
  waiting for transfers between devices: 55.4 us -> 44.6 us
    all_gather x2, waiting for transfers between devices: 20.5 us -> 13.7 us  [on_device_pairs(): lax.all_gather(piece, 'shard', axis=0, tiled=False)]
    ppermute x2, starting transfers between devices: 8.13 us -> 14.1 us  [on_device_pairs(): sent = lax.ppermute(theirs, 'group', swap)]
    ppermute x2, waiting for transfers between devices: 12.6 us -> 6.98 us  [on_device_pairs(): sent = lax.ppermute(theirs, 'group', swap)]
    ppermute x2, starting transfers between devices: 13.8 us -> 8.62 us  [on_device_pairs(): other = lax.ppermute(held, 'shard', [(i, i ^ bit) for i in range(shards)])]
  transfers between devices with their start and end apart: 18 -> 18, of which waited for: 7 -> 7; matrix products, arithmetic and copies ran while one was open for 45% -> 47% of each run, Pallas kernels for 0% -> 0%
where the time goes in v2:
time: 212 us; the launch traced here: 209 us
  other arithmetic  56.9 us (27%)
  waiting for transfers between devices  44.6 us (21%)
  starting transfers between devices  40.3 us (19%)
  matrix products  39.8 us (19%)
  between operations  15.9 us (8%)
  local copies, waits for them, and re-layouts  11.7 us (6%)
    another operation x6, other arithmetic, solve_spd(): lower_factor = jnp.linalg.cholesky(pivot_block)  24.8 us
    another operation x4, other arithmetic, solve_spd(): lax.linalg.triangular_solve(lower_factor, half_solved, left_side=True, lo...  21 us
    dot_general x2, matrix products, on_device_pairs(): lax.dot_general(half_swept, piece, (((1,), (1,)), ((), ())), preferred_el...  18.8 us
    ppermute x2, starting transfers between devices, on_device_pairs(): sent = lax.ppermute(theirs, 'group', swap)  14.1 us
    all_gather x2, waiting for transfers between devices, on_device_pairs(): lax.all_gather(piece, 'shard', axis=0, tiled=False)  13.7 us
    ppermute x3, waiting for transfers between devices, on_device_pairs(): lax.ppermute(tops, 'shard', tree)  10.3 us
    dot_general x6, matrix products, exact(): jnp.dot(a, b, precision=lax.Precision.HIGHEST, preferred_element_type=jnp...  9.32 us
    ppermute x2, starting transfers between devices, on_device_pairs(): other = lax.ppermute(held, 'shard', [(i, i ^ bit) for i in range(shards)])  8.62 us
  transfers between devices with their start and end apart: 18, of which 7 were waited for; matrix products, arithmetic and copies ran while one was open for 47% of the time, Pallas kernels for 0%

profile of v2, /device:TPU:0, one launch (start us, length us, event | category | flops | bytes accessed | tf_op | source)
XLA Modules:
  0.0 209.2 jit_solution(12835110061722533865)
XLA Ops:
  7.2 2.1 slice.157
  10.4 3.1 %collective-permute-start.4 = (bf16[128,512]{0,1:T(8,128)(2,1)S(1)}, bf16[128,512]{0,1:T(8,128)(2,1)S(1)}, u32[]{:S(2)}, u32[]{:S(2)}) collective-permute-start(bf16[128,512]{0,1:T(8,128)(2,1)S(1)} %bitcast_convert_fusion), channel_id=1, source_target_pairs={{0,16},{16,0},{1,17},{17,1},{2,18},{18,2},{3,19},{19,3},{4,20},{20... | collective-permute-start | bytes 393224 | tf_op jit(solution)/shard_map/ppermute | solution.py:127
  13.4 2.6 %collective-permute-start = (bf16[2,8192]{1,0:T(2,128)(2,1)S(1)}, bf16[2,8192]{1,0:T(2,128)(2,1)S(1)}, u32[]{:S(2)}, u32[]{:S(2)}) collective-permute-start(bf16[2,8192]{1,0:T(2,128)(2,1)S(1)} %copy-done.3), channel_id=1, source_target_pairs={{0,8},{1,9},{2,10},{3,11},{4,12},{5,13},{6,14},{7,15},{8,0},{9,1},... | collective-permute-start | bytes 98312 | tf_op jit(solution)/shard_map/ppermute | solution.py:120
  16.6 1.7 slice.158
  18.4 3.4 %compare_select_fusion = f32[256,4096]{0,1:T(8,128)} fusion(s32[256]{0:T(256)S(1)} %pad_add_fusion, s32[4096]{0:T(1024)S(1)} %iota_add_fusion), kind=kLoop, calls=%fused_computation.2 | loop fusion | flops 2097152 | bytes 4211712 | tf_op jit(solution)/shard_map/jit(_where)/select_n | solution.py:154
  22.5 1.6 collective-permute-start.1
  24.2 2.2 %collective-permute-start.6 = (bf16[2,256,128]{1,2,0:T(8,128)(2,1)S(1)}, bf16[2,256,128]{1,2,0:T(8,128)(2,1)S(1)}, u32[]{:S(2)}, u32[]{:S(2)}) collective-permute-start(bf16[2,256,128]{1,2,0:T(8,128)(2,1)S(1)} %pad_maximum_fusion.7), channel_id=1, source_target_pairs={{0,8},{8,0},{16,24},{24,16}} | collective-permute-start | bytes 393224 | tf_op jit(solution)/shard_map/ppermute | solution.py:119
  26.5 4.4 %collective-permute-done.1 = bf16[4,8192]{1,0:T(4,128)(2,1)S(1)} collective-permute-done((bf16[4,8192]{1,0:T(4,128)(2,1)S(1)}, bf16[4,8192]{1,0:T(4,128)(2,1)S(1)}, u32[]{:S(2)}, u32[]{:S(2)}) %collective-permute-start.1) | collective-permute-done | bytes 65568 | tf_op jit(solution)/shard_map/ppermute | solution.py:124
  31.0 1.9 collective-permute-start.2
  34.3 4.9 %collective-permute-done.6 = bf16[2,256,128]{1,2,0:T(8,128)(2,1)S(1)} collective-permute-done((bf16[2,256,128]{1,2,0:T(8,128)(2,1)S(1)}, bf16[2,256,128]{1,2,0:T(8,128)(2,1)S(1)}, u32[]{:S(2)}, u32[]{:S(2)}) %collective-permute-start.6) | collective-permute-done | bytes 131104 | tf_op jit(solution)/shard_map/ppermute | solution.py:119
  40.9 4.2 %collective-permute-done.10 = bf16[256,512]{0,1:T(8,128)(2,1)S(1)} collective-permute-done((bf16[256,512]{0,1:T(8,128)(2,1)S(1)}, bf16[256,512]{0,1:T(8,128)(2,1)S(1)}, u32[]{:S(2)}, u32[]{:S(2)}) %collective-permute-start.10) | collective-permute-done | bytes 262176 | tf_op jit(solution)/shard_map/ppermute | solution.py:130
  45.7 7.8 %collective-permute-done.7 = bf16[2,256,256]{1,2,0:T(8,128)(2,1)S(1)} collective-permute-done((bf16[2,256,256]{1,2,0:T(8,128)(2,1)S(1)}, bf16[2,256,256]{1,2,0:T(8,128)(2,1)S(1)}, u32[]{:S(2)}, u32[]{:S(2)}) %collective-permute-start.7) | collective-permute-done | bytes 262176 | tf_op jit(solution)/shard_map/ppermute | solution.py:123
  56.3 2.5 %collective-permute-done.8 = bf16[2,256,256]{1,2,0:T(8,128)(2,1)S(1)} collective-permute-done((bf16[2,256,256]{1,2,0:T(8,128)(2,1)S(1)}, bf16[2,256,256]{1,2,0:T(8,128)(2,1)S(1)}, u32[]{:S(2)}, u32[]{:S(2)}) %collective-permute-start.8) | collective-permute-done | bytes 262176 | tf_op jit(solution)/shard_map/ppermute | solution.py:123
  60.4 8.1 %collective-permute-start.12 = (bf16[256,1024]{0,1:T(8,128)(2,1)S(1)}, bf16[256,1024]{0,1:T(8,128)(2,1)S(1)}, u32[]{:S(2)}, u32[]{:S(2)}) collective-permute-start(bf16[256,1024]{0,1:T(8,128)(2,1)S(1)} %pad_maximum_fusion.2), channel_id=1, source_target_pairs={{0,4},{1,5},{2,6},{3,7},{4,0},{5,1},{6,2},{7,3},{8,12},{9,13},{10,... | collective-permute-start | bytes 1572872 | tf_op jit(solution)/shard_map/ppermute | solution.py:133
  69.0 11.7 %cholesky.44 = f32[128,128]{1,0:T(8,128)S(1)} custom-call(f32[128,128]{1,0:T(8,128)S(1)} %fusion.41), custom_call_target="Cholesky" | custom-call | tf_op jit(solution)/shard_map/jit(cholesky)/cholesky | solution.py:20
  82.0 9.8 %custom-call.11 = f32[1,128,128]{1,2,0:T(8,128)S(1)} custom-call(f32[1,128,128]{2,1,0:T(8,128)S(1)} %fusion.28), custom_call_target="InvertDiagBlocksLowerTriangular" | custom-call | tf_op jit(solution)/shard_map/triangular_solve/custom-call.2 | solution.py:22
  93.7 11.7 %cholesky.55 = f32[128,128]{1,0:T(8,128)S(1)} custom-call(f32[128,128]{1,0:T(8,128)S(1)} %fusion.37), custom_call_target="Cholesky" | custom-call | tf_op jit(solution)/shard_map/jit(cholesky)/cholesky | solution.py:20
  107.9 10.0 %custom-call.13 = f32[1,128,128]{1,2,0:T(8,128)S(1)} custom-call(f32[1,128,128]{2,1,0:T(8,128)S(1)} %fusion.29), custom_call_target="InvertDiagBlocksLowerTriangular" | custom-call | tf_op jit(solution)/shard_map/triangular_solve/custom-call.2 | solution.py:22
  123.2 1.9 fusion.7
  125.0 3.6 %fusion = f32[128,4096]{0,1:T(8,128)S(1)} fusion(f32[128,4096]{1,0:T(8,128)S(1)} %fusion.7, f32[256,4096]{0,1:T(8,128)S(1)} %copy-done, f32[256,4096]{0,1:T(8,128)S(1)} %fusion.1, f32[256,256]{0,1:T(8,128)S(1)} %fusion.16), kind=kOutput, calls=%fused_computation.5 | convolution fusion | flops 806354944 | bytes 8454144 | tf_op jit(solution)/shard_map/dot_general | solution.py:92
  128.7 2.0 fusion.59
  130.7 4.2 %fusion.2 = f32[512,4096]{1,0:T(8,128)S(1)} fusion(f32[128,4096]{1,0:T(8,128)S(1)} %fusion.59, f32[128,4096]{1,0:T(8,128)S(1)} %fusion.7, f32[512,128]{1,0:T(8,128)S(1)} %fusion.30, f32[512,128]{1,0:T(8,128)S(1)} %slice-done.2), kind=kOutput, calls=%fused_computation.7 | convolution fusion | flops 3222405120 | bytes 13107200 | tf_op jit(solution)/shard_map/dot_general | solution.py:170
  134.9 4.8 %add_subtract_fusion = f32[512,4096]{1,0:T(8,128)} fusion(f32[512,4096]{1,0:T(8,128)S(1)} %fusion.2, f32[512,4096]{1,0:T(8,128)S(1)} %bitcast.60, f32[]{:T(128)} %bitcast.55, s32[4096]{0:T(1024)S(1)} %iota_add_fusion, s32[512]{0:T(512)S(1)} %copy-done.12, bf16[32,8192]{1,0:T(8,128)(2,1)S(1)} %concatenate.55, s32[]{:T(128)S(6)} %select_n.187, s32[]{:T(128)S(6)} %select_n.186), kind=kOutput, calls=%fused_computation | convolution fusion | flops 148897792 | bytes 25479180 | tf_op jit(solution)/shard_map/dot_general | solution.py:87
  139.7 3.5 %fusion.6 = f32[512,4096]{1,0:T(8,128)} fusion(f32[512,4096]{1,0:T(8,128)} %add_subtract_fusion, f32[128,4096]{1,0:T(8,128)S(1)} %fusion.7, f32[128,4096]{1,0:T(8,128)S(1)} %fusion.59, pred[]{:T(512)S(6)} %eq.128, pred[]{:T(512)S(6)} %eq.120), kind=kLoop, calls=%fused_computation.12 | loop fusion | flops 1572864 | bytes 8388610 | tf_op jit(solution)/shard_map/scatter-add | solution.py:173
  143.2 11.8 %fusion.11 = f32[512,1536]{1,0:T(8,128)S(1)} fusion(bf16[1536,4096]{1,0:T(8,128)(2,1)} %all-gather.5.cloned.1.call-done, f32[512,4096]{1,0:T(8,128)} %fusion.6), kind=kOutput, calls=%fused_computation.18 | convolution fusion | flops 6444548096 | bytes 24117248 | tf_op jit(solution)/shard_map/dot_general | solution.py:179
  155.0 1.6 copy-done.1
  156.8 12.6 %collective-permute-start.14 = (bf16[512,768]{1,0:T(8,128)(2,1)S(1)}, bf16[512,768]{1,0:T(8,128)(2,1)S(1)}, u32[]{:S(2)}, u32[]{:S(2)}) collective-permute-start(bf16[512,768]{1,0:T(8,128)(2,1)S(1)} %dynamic-slice_convert_fusion), channel_id=1, source_target_pairs={{0,16},{16,0},{1,17},{17,1},{2,18},{18,2},{3,19},{19,3},{4,20},{20... | collective-permute-start | bytes 2359304 | tf_op jit(solution)/shard_map/ppermute | solution.py:181
  169.3 13.7 %all-gather.7.cloned.1.call-done = bf16[512,4096]{1,0:T(8,128)(2,1)} async-done(((bf16[32,4096]{1,0:T(8,128)(2,1)}), bf16[512,4096]{1,0:T(8,128)(2,1)}) %all-gather.7.cloned.1.call-update) | async-done | bytes 4194320 | tf_op jit(solution)/shard_map/all_gather | solution.py:140
  183.0 6.9 %fusion.9 = f32[512,512]{0,1:T(8,128)S(1)} fusion(bf16[512,4096]{1,0:T(8,128)(2,1)} %all-gather.7.cloned.1.call-done, f32[512,4096]{1,0:T(8,128)} %fusion.6), kind=kOutput, calls=%fused_computation.16 | convolution fusion | flops 2149580800 | bytes 13631488 | tf_op jit(solution)/shard_map/dot_general | solution.py:179
  190.0 1.5 collective-permute-start.15
  191.6 7.0 %collective-permute-done.15 = bf16[512,256]{0,1:T(8,128)(2,1)S(1)} collective-permute-done((bf16[512,256]{0,1:T(8,128)(2,1)S(1)}, bf16[512,256]{0,1:T(8,128)(2,1)S(1)}, u32[]{:S(2)}, u32[]{:S(2)}) %collective-permute-start.15) | collective-permute-done | bytes 262176 | tf_op jit(solution)/shard_map/ppermute | solution.py:181
  198.6 1.6 add_convert_fusion
  (126 shorter events, 22.9 us)
Async XLA Ops:
  7.2 6.3 %copy-start.3 = (bf16[2,8192]{1,0:T(2,128)(2,1)S(1)}, bf16[2,8192]{1,0:T(2,128)(2,1)}, u32[]{:S(2)}) copy-start(bf16[2,8192]{1,0:T(2,128)(2,1)} %param.13) | copy-start | bytes 98308
  7.2 136.0 %all-gather.5.cloned.1.call-start = ((), (), s32[]{:S(2)}) async-start(), calls=%async_computation | async-start | bytes 13369344 | tf_op jit(solution)/shard_map/all_gather | solution.py:140
  9.3 173.7 %all-gather.7.cloned.1.call-start = ((), (), s32[]{:S(2)}) async-start(), calls=%async_computation.1 | async-start | bytes 4456448 | tf_op jit(solution)/shard_map/all_gather | solution.py:140
  10.4 22.5 %collective-permute-start.4 = (bf16[128,512]{0,1:T(8,128)(2,1)S(1)}, bf16[128,512]{0,1:T(8,128)(2,1)S(1)}, u32[]{:S(2)}, u32[]{:S(2)}) collective-permute-start(bf16[128,512]{0,1:T(8,128)(2,1)S(1)} %bitcast_convert_fusion), channel_id=1, source_target_pairs={{0,16},{16,0},{1,17},{17,1},{2,18},{18,2},{3,19},{19,3},{4,20},{20... | collective-permute-start | bytes 393224 | tf_op jit(solution)/shard_map/ppermute | solution.py:127
  13.4 9.0 %collective-permute-start = (bf16[2,8192]{1,0:T(2,128)(2,1)S(1)}, bf16[2,8192]{1,0:T(2,128)(2,1)S(1)}, u32[]{:S(2)}, u32[]{:S(2)}) collective-permute-start(bf16[2,8192]{1,0:T(2,128)(2,1)S(1)} %copy-done.3), channel_id=1, source_target_pairs={{0,8},{1,9},{2,10},{3,11},{4,12},{5,13},{6,14},{7,15},{8,0},{9,1},... | collective-permute-start | bytes 98312 | tf_op jit(solution)/shard_map/ppermute | solution.py:120
  16.1 8.1 %collective-permute-start.5 = (bf16[2,128,128]{1,2,0:T(8,128)(2,1)S(1)}, bf16[2,128,128]{1,2,0:T(8,128)(2,1)S(1)}, u32[]{:S(2)}, u32[]{:S(2)}) collective-permute-start(bf16[2,128,128]{1,2,0:T(8,128)(2,1)S(1)} %pad_maximum_fusion.9), channel_id=1, source_target_pairs={{0,16},{16,0},{1,17},{17,1},{2,18},{18,2},{3,19},{19,3},{4,20},{20... | collective-permute-start | bytes 196616 | tf_op jit(solution)/shard_map/ppermute | solution.py:117
  18.4 50.2 %copy-start.13 = (s32[256]{0:T(256)}, s32[256]{0:T(256)S(1)}, u32[]{:S(2)}) copy-start(s32[256]{0:T(256)S(1)} %pad_add_fusion) | copy-start | bytes 3076
  21.8 33.5 %copy-start.11 = (s32[512]{0:T(512)}, s32[512]{0:T(512)S(1)}, u32[]{:S(2)}) copy-start(s32[512]{0:T(512)S(1)} %iota_add_fusion.1) | copy-start | bytes 6148
  22.5 8.3 %collective-permute-start.1 = (bf16[4,8192]{1,0:T(4,128)(2,1)S(1)}, bf16[4,8192]{1,0:T(4,128)(2,1)S(1)}, u32[]{:S(2)}, u32[]{:S(2)}) collective-permute-start(bf16[4,8192]{1,0:T(4,128)(2,1)S(1)} %pad_maximum_fusion.8), channel_id=1, source_target_pairs={{0,4},{1,5},{2,6},{3,7},{4,0},{5,1},{6,2},{7,3},{8,12},{9,13},{10,... | collective-permute-start | bytes 196616 | tf_op jit(solution)/shard_map/ppermute | solution.py:124
  24.2 15.0 %collective-permute-start.6 = (bf16[2,256,128]{1,2,0:T(8,128)(2,1)S(1)}, bf16[2,256,128]{1,2,0:T(8,128)(2,1)S(1)}, u32[]{:S(2)}, u32[]{:S(2)}) collective-permute-start(bf16[2,256,128]{1,2,0:T(8,128)(2,1)S(1)} %pad_maximum_fusion.7), channel_id=1, source_target_pairs={{0,8},{8,0},{16,24},{24,16}} | collective-permute-start | bytes 393224 | tf_op jit(solution)/shard_map/ppermute | solution.py:119
  31.0 9.6 %collective-permute-start.2 = (bf16[8,8192]{1,0:T(8,128)(2,1)S(1)}, bf16[8,8192]{1,0:T(8,128)(2,1)S(1)}, u32[]{:S(2)}, u32[]{:S(2)}) collective-permute-start(bf16[8,8192]{1,0:T(8,128)(2,1)S(1)} %pad_maximum_fusion.6), channel_id=1, source_target_pairs={{0,2},{1,3},{2,0},{3,1},{4,6},{5,7},{6,4},{7,5},{8,10},{9,11},{10,... | collective-permute-start | bytes 393224 | tf_op jit(solution)/shard_map/ppermute | solution.py:124
  32.9 12.2 %collective-permute-start.10 = (bf16[256,512]{0,1:T(8,128)(2,1)S(1)}, bf16[256,512]{0,1:T(8,128)(2,1)S(1)}, u32[]{:S(2)}, u32[]{:S(2)}) collective-permute-start(bf16[256,512]{0,1:T(8,128)(2,1)S(1)} %pad_maximum_fusion.4), channel_id=1, source_target_pairs={{0,8},{1,9},{2,10},{3,11},{4,12},{5,13},{6,14},{7,15},{24,16},{25,... | collective-permute-start | bytes 786440 | tf_op jit(solution)/shard_map/ppermute | solution.py:130
  39.3 14.3 %collective-permute-start.7 = (bf16[2,256,256]{1,2,0:T(8,128)(2,1)S(1)}, bf16[2,256,256]{1,2,0:T(8,128)(2,1)S(1)}, u32[]{:S(2)}, u32[]{:S(2)}) collective-permute-start(bf16[2,256,256]{1,2,0:T(8,128)(2,1)S(1)} %pad_maximum_fusion.5), channel_id=1, source_target_pairs={{0,4},{8,12},{16,20},{24,28}} | collective-permute-start | bytes 786440 | tf_op jit(solution)/shard_map/ppermute | solution.py:123
  40.8 14.1 %collective-permute-start.3 = (bf16[16,8192]{1,0:T(8,128)(2,1)S(1)}, bf16[16,8192]{1,0:T(8,128)(2,1)S(1)}, u32[]{:S(2)}, u32[]{:S(2)}) collective-permute-start(bf16[16,8192]{1,0:T(8,128)(2,1)S(1)} %pad_maximum_fusion.3), channel_id=1, source_target_pairs={{0,1},{1,0},{2,3},{3,2},{4,5},{5,4},{6,7},{7,6},{8,9},{9,8},{10,11... | collective-permute-start | bytes 786440 | tf_op jit(solution)/shard_map/ppermute | solution.py:124
  45.2 15.1 %collective-permute-start.11 = (bf16[256,512]{0,1:T(8,128)(2,1)S(1)}, bf16[256,512]{0,1:T(8,128)(2,1)S(1)}, u32[]{:S(2)}, u32[]{:S(2)}) collective-permute-start(bf16[256,512]{0,1:T(8,128)(2,1)S(1)} %broadcast_select_fusion.4), channel_id=1, source_target_pairs={{0,2},{1,3},{2,0},{3,1},{4,6},{5,7},{6,4},{7,5},{8,10},{9,11},{10,... | collective-permute-start | bytes 786440 | tf_op jit(solution)/shard_map/ppermute | solution.py:133
  53.6 5.2 %collective-permute-start.8 = (bf16[2,256,256]{1,2,0:T(8,128)(2,1)S(1)}, bf16[2,256,256]{1,2,0:T(8,128)(2,1)S(1)}, u32[]{:S(2)}, u32[]{:S(2)}) collective-permute-start(bf16[2,256,256]{1,2,0:T(8,128)(2,1)S(1)} %broadcast_select_fusion.7), channel_id=1, source_target_pairs={{0,2},{4,6},{8,10},{12,14},{16,18},{20,22},{24,26},{28,30}} | collective-permute-start | bytes 786440 | tf_op jit(solution)/shard_map/ppermute | solution.py:123
  55.2 13.6 %copy-start.7 = (bf16[32,128]{1,0:T(8,128)(2,1)}, bf16[32,128]{1,0:T(8,128)(2,1)S(1)}, u32[]{:S(2)}) copy-start(bf16[32,128]{1,0:T(8,128)(2,1)S(1)} %get-tuple-element.37) | copy-start | bytes 24580
  55.2 13.6 %copy-start.9 = (bf16[32,128]{1,0:T(8,128)(2,1)}, bf16[32,128]{1,0:T(8,128)(2,1)S(1)}, u32[]{:S(2)}) copy-start(bf16[32,128]{1,0:T(8,128)(2,1)S(1)} %get-tuple-element.38) | copy-start | bytes 24580
  55.5 0.8 copy-start.2
  58.8 9.7 %collective-permute-start.9 = (bf16[2,256,256]{1,2,0:T(8,128)(2,1)S(1)}, bf16[2,256,256]{1,2,0:T(8,128)(2,1)S(1)}, u32[]{:S(2)}, u32[]{:S(2)}) collective-permute-start(bf16[2,256,256]{1,2,0:T(8,128)(2,1)S(1)} %broadcast_select_fusion.8), channel_id=1, source_target_pairs={{0,1},{2,3},{4,5},{6,7},{8,9},{10,11},{12,13},{14,15},{16,17},{18,... | collective-permute-start | bytes 786440 | tf_op jit(solution)/shard_map/ppermute | solution.py:123
  60.4 45.6 %collective-permute-start.12 = (bf16[256,1024]{0,1:T(8,128)(2,1)S(1)}, bf16[256,1024]{0,1:T(8,128)(2,1)S(1)}, u32[]{:S(2)}, u32[]{:S(2)}) collective-permute-start(bf16[256,1024]{0,1:T(8,128)(2,1)S(1)} %pad_maximum_fusion.2), channel_id=1, source_target_pairs={{0,4},{1,5},{2,6},{3,7},{4,0},{5,1},{6,2},{7,3},{8,12},{9,13},{10,... | collective-permute-start | bytes 1572872 | tf_op jit(solution)/shard_map/ppermute | solution.py:133
  106.1 1.2 copy-start.6
  106.2 13.6 %copy-start.4 = (f32[128,128]{1,0:T(8,128)S(1)}, f32[128,128]{1,0:T(8,128)}, u32[]{:S(2)}) copy-start(f32[128,128]{1,0:T(8,128)} %copy.19) | copy-start | bytes 196612
  107.3 12.5 %collective-permute-start.13 = (bf16[256,2048]{0,1:T(8,128)(2,1)}, bf16[256,2048]{0,1:T(8,128)(2,1)S(1)}, u32[]{:S(2)}, u32[]{:S(2)}) collective-permute-start(bf16[256,2048]{0,1:T(8,128)(2,1)} %pad_maximum_fusion), channel_id=1, source_target_pairs={{0,1},{1,0},{2,3},{3,2},{4,5},{5,4},{6,7},{7,6},{8,9},{9,8},{10,11... | collective-permute-start | bytes 3145736 | tf_op jit(solution)/shard_map/ppermute | solution.py:135
  121.0 2.2 %copy-start = (f32[256,4096]{0,1:T(8,128)S(1)}, f32[256,4096]{0,1:T(8,128)}, u32[]{:S(2)}) copy-start(f32[256,4096]{0,1:T(8,128)} %compare_select_fusion) | copy-start | bytes 12582916
  125.0 5.6 %slice-start.2 = ((f32[512,256]{1,0:T(8,128)}), f32[512,128]{1,0:T(8,128)S(1)}, s32[]{:S(2)}) async-start(f32[512,256]{1,0:T(8,128)} %copy-done.2), calls=%async_computation.4 | async-start | bytes 524288 | tf_op jit(solution)/shard_map/slice | solution.py:168
  128.7 6.2 %slice-start = ((s8[8388608]{0:T(1024)(128)(4,1)}), s8[4194304]{0:T(1024)(128)(4,1)S(1)}, s32[]{:S(2)}) async-start(s8[8388608]{0:T(1024)(128)(4,1)} %bitcast.59), calls=%async_computation.2 | async-start | bytes 8388608
  130.7 4.2 %slice-start.1 = ((s8[8388608]{0:T(1024)(128)(4,1)}), s8[4194304]{0:T(1024)(128)(4,1)S(1)}, s32[]{:S(2)}) async-start(s8[8388608]{0:T(1024)(128)(4,1)} %bitcast.59), calls=%async_computation.3 | async-start | bytes 8388608
  130.7 4.2 %copy-start.12 = (s32[512]{0:T(512)S(1)}, s32[512]{0:T(512)}, u32[]{:S(2)}) copy-start(s32[512]{0:T(512)} %copy-done.11) | copy-start | bytes 6148
  155.0 1.6 copy-start.1
  156.8 41.8 %collective-permute-start.14 = (bf16[512,768]{1,0:T(8,128)(2,1)S(1)}, bf16[512,768]{1,0:T(8,128)(2,1)S(1)}, u32[]{:S(2)}, u32[]{:S(2)}) collective-permute-start(bf16[512,768]{1,0:T(8,128)(2,1)S(1)} %dynamic-slice_convert_fusion), channel_id=1, source_target_pairs={{0,16},{16,0},{1,17},{17,1},{2,18},{18,2},{3,19},{19,3},{4,20},{20... | collective-permute-start | bytes 2359304 | tf_op jit(solution)/shard_map/ppermute | solution.py:181
  190.0 8.5 %collective-permute-start.15 = (bf16[512,256]{0,1:T(8,128)(2,1)S(1)}, bf16[512,256]{0,1:T(8,128)(2,1)S(1)}, u32[]{:S(2)}, u32[]{:S(2)}) collective-permute-start(bf16[512,256]{0,1:T(8,128)(2,1)S(1)} %dynamic-slice_convert_fusion.1), channel_id=1, source_target_pairs={{0,16},{16,0},{1,17},{17,1},{2,18},{18,2},{3,19},{19,3},{4,20},{20... | collective-permute-start | bytes 786440 | tf_op jit(solution)/shard_map/ppermute | solution.py:181
  (4 other events, 2.9 us)
Sparse Core Ops, SparseCore 0:
  10.3 116.5 all-gather.4
  129.0 53.9 all-gather.6
